TPU v7x, 256 devices: a whole 4x4x8 slice. The times are simulated.
256 devices in a mesh: dp: 2 (over x_hi), lat: 16 (over x_lo, z), lon: 8 (over y, core).
Axes of the slice: x: 4 (x_hi: 2, x_lo: 2; x = x_hi * 2 + x_lo), y: 4, z: 8, core: 2. Of those that a mesh axis runs over, the one named last changes fastest.
Arguments:
- hidden_in: bfloat16 [2, 480, 480, 384], P('dp', 'lat', 'lon'), may hold values from -6 to 6
- grad_out: bfloat16 [2, 480, 480, 384], P('dp', 'lat', 'lon'), may hold values from -6 to 6
- norm_gain: float32 [384], replicated, may hold values from 0.5 to 1.5
- w_qkv: bfloat16 [384, 1152], replicated, may hold values from -0.3125 to 0.3125
- w_proj: bfloat16 [384, 384], replicated, may hold values from -0.3125 to 0.3125
Outputs:
- grad_in: bfloat16 [2, 480, 480, 384], P('dp', 'lat', 'lon')
- grad_qkv: float32 [384, 1152], P('dp', ('lat', 'lon'))
- grad_proj: float32 [384, 384], P('dp', ('lat', 'lon'))
All inputs are finite; a program needn't handle non-finite values.
Results may differ from a plain program's by a relative error of at most 0.0083.
Values may be sent and summed in bfloat16 or wider, within the bound.
A program may use at most 64 MiB of HBM per device.

v0:
```python
import jax
import jax.numpy as jnp
from jax import lax
from jax.sharding import Mesh
from jax.sharding import PartitionSpec as P

HEADS = 6
WIN = 30
SHIFT = 15
LON = ("lon_0", "lon_1")
LAT = ("lat_0", "lat_1")
LAT_LON = ("lat_0", "lat_1", "lon_0", "lon_1")


EPSILON = 1e-05


def shifted_2(value, axis, steps):
    count = lax.axis_size(axis)
    pairs = [(source, (source + steps) % count) for source in range(count)]
    return lax.ppermute(value, axis, pairs)


def passed_along(x, axis, by):
    peers = lax.axis_size(axis)
    pairs = [(i, i + by) for i in range(peers) if 0 <= i + by < peers]
    return lax.ppermute(x, axis, pairs)


def split_up(x, dim, peers):
    dims = x.shape
    pieces = x.reshape(*dims[:dim], peers, dims[dim] // peers, *dims[dim + 1 :])
    return jnp.moveaxis(pieces, dim, 0)


def scatter_pairs(x, chips, core, dim):
    sizes = (lax.axis_size(chips), lax.axis_size(core))
    pieces = split_up(x, dim, sizes[0] * sizes[1])
    inside = pieces.shape[1:]
    pieces = pieces.reshape(*sizes, *inside).swapaxes(0, 1).reshape(-1, *inside)
    pieces = lax.psum_scatter(pieces, core, scatter_dimension=0, tiled=True)
    return lax.psum_scatter(pieces, chips, scatter_dimension=0, tiled=True)[0]


def in_one_piece(arrays, axis, dim, along):
    both = jnp.concatenate(arrays, axis=along)
    out, at, outs = (lax.psum_scatter(both, axis, scatter_dimension=dim, tiled=True), 0, [])
    for a in arrays:
        outs.append(lax.slice_in_dim(out, at, at + a.shape[along], axis=along))
        at += a.shape[along]
    return tuple(outs)


def attend_head(query_rows, key_rows, value_rows, grad_rows, key_valid, scaling):
    scores = jnp.dot(query_rows, key_rows.T, preferred_element_type=jnp.float32) * scaling
    weights_raw = jnp.exp(scores) * key_valid[None, :]
    attention = weights_raw / jnp.sum(weights_raw, axis=-1, keepdims=True)
    attention_low = attention.astype(jnp.bfloat16)
    outputs = jnp.dot(attention_low, value_rows, preferred_element_type=jnp.float32).astype(
        jnp.bfloat16
    )
    dprobs = jnp.dot(grad_rows, value_rows.T, preferred_element_type=jnp.float32)
    row_total = jnp.sum(attention * dprobs, axis=-1, keepdims=True)
    dscores = (attention * (dprobs - row_total) * scaling).astype(jnp.bfloat16)
    dquery = jnp.dot(dscores, key_rows, preferred_element_type=jnp.float32).astype(jnp.bfloat16)
    dkey_rows = jnp.dot(dscores.T, query_rows, preferred_element_type=jnp.float32).astype(
        jnp.bfloat16
    )
    dvalue = jnp.dot(attention_low.T, grad_rows, preferred_element_type=jnp.float32).astype(
        jnp.bfloat16
    )
    return (outputs, dquery, dkey_rows, dvalue)


def window_grads(window_cells, cotangent, key_valid, norm_gain, w_qkv, w_proj):
    model_width = window_cells.shape[1]
    head_size = model_width // HEADS
    scaling = head_size ** (-0.5)
    values_f = window_cells.astype(jnp.float32)
    average = jnp.mean(values_f, axis=1, keepdims=True)
    centred = values_f - average
    inverse_std = lax.rsqrt(jnp.mean(centred * centred, axis=1, keepdims=True) + EPSILON)
    normed = centred * inverse_std
    normal_low = (normed * norm_gain).astype(jnp.bfloat16)
    qkv = jnp.dot(normal_low, w_qkv, preferred_element_type=jnp.float32).astype(jnp.bfloat16)
    back_rows = jnp.dot(cotangent, w_proj.T, preferred_element_type=jnp.float32).astype(
        jnp.bfloat16
    )

    def split_heads(matrix):
        return matrix.reshape(matrix.shape[0], HEADS, head_size).transpose(1, 0, 2)

    def merge_heads(stacked):
        return stacked.transpose(1, 0, 2).reshape(stacked.shape[1], model_width)

    def one_head(inputs):
        return attend_head(inputs[0], inputs[1], inputs[2], inputs[3], key_valid, scaling)

    heads_in = (
        split_heads(qkv[:, :model_width]),
        split_heads(qkv[:, model_width : 2 * model_width]),
        split_heads(qkv[:, 2 * model_width :]),
        split_heads(back_rows),
    )
    outputs, dquery, dkey_rows, dvalue = lax.map(one_head, heads_in)
    attended = merge_heads(outputs)
    dqkv = jnp.concatenate(
        [merge_heads(dquery), merge_heads(dkey_rows), merge_heads(dvalue)], axis=1
    )
    proj_part = jnp.dot(attended.T, cotangent, preferred_element_type=jnp.float32)
    qkv_part = jnp.dot(normal_low.T, dqkv, preferred_element_type=jnp.float32)
    dnormed = jnp.dot(dqkv, w_qkv.T, preferred_element_type=jnp.float32) * norm_gain
    dcells = inverse_std * (
        dnormed
        - jnp.mean(dnormed, axis=1, keepdims=True)
        - normed * jnp.mean(dnormed * normed, axis=1, keepdims=True)
    )
    return (dcells.astype(jnp.bfloat16), qkv_part, proj_part)


def to_windows(grid_field):
    shape = grid_field.shape
    split = grid_field.reshape(shape[0], shape[1] // WIN, WIN, shape[2] // WIN, WIN, shape[3])
    return split.transpose(0, 1, 3, 2, 4, 5).reshape(-1, WIN * WIN, shape[3])


def from_windows(windows, samples, lat_rows, lon_cols):
    split = windows.reshape(samples, lat_rows // WIN, lon_cols // WIN, WIN, WIN, windows.shape[-1])
    return split.transpose(0, 1, 3, 2, 4, 5).reshape(samples, lat_rows, lon_cols, windows.shape[-1])


def ahead_lon(stacked):
    outgoing = stacked[:, :, :SHIFT]
    incoming = shifted_2(outgoing, LON, -1)
    return jnp.concatenate([stacked[:, :, SHIFT:], incoming], axis=2)


def ahead_lat(stacked):
    outgoing = stacked[:, :SHIFT]
    incoming = passed_along(outgoing, LAT, -1)
    return jnp.concatenate([stacked[:, SHIFT:], incoming], axis=1)


def behind_lon(stacked):
    outgoing = stacked[:, :, -SHIFT:]
    incoming = shifted_2(outgoing, LON, 1)
    return jnp.concatenate([incoming, stacked[:, :, :-SHIFT]], axis=2)


def behind_lat(stacked):
    outgoing = stacked[:, -SHIFT:]
    incoming = passed_along(outgoing, LAT, 1)
    return jnp.concatenate([incoming, stacked[:, :-SHIFT]], axis=1)


def per_device(hidden_in, grad_out, norm_gain, w_qkv, w_proj):
    samples, lat_rows, lon_cols, model_width = hidden_in.shape
    stacked = jnp.concatenate([hidden_in, grad_out], axis=0)
    stacked = ahead_lon(ahead_lat(stacked))
    shifted = stacked[:samples]
    cotangent = stacked[samples:]
    grid_rows = lat_rows * lax.axis_size(LAT)
    row_index = lax.axis_index(LAT) * lat_rows + jnp.arange(lat_rows, dtype=jnp.int32)
    valid_rows = (row_index < grid_rows - SHIFT).astype(jnp.float32)
    valid_field = jnp.broadcast_to(
        valid_rows[None, :, None, None], (samples, lat_rows, lon_cols, 1)
    )
    valid_windows = to_windows(valid_field)[..., 0]

    def step_window(totals, inputs):
        dcells, qkv_part, proj_part = window_grads(
            inputs[0], inputs[1], inputs[2], norm_gain, w_qkv, w_proj
        )
        return ((totals[0] + qkv_part, totals[1] + proj_part), dcells)

    starting = (
        jnp.zeros((model_width, 3 * model_width), jnp.float32),
        jnp.zeros((model_width, model_width), jnp.float32),
    )
    sums, dwindows = lax.scan(
        step_window, starting, (to_windows(shifted), to_windows(cotangent), valid_windows)
    )
    dshift = from_windows(dwindows, samples, lat_rows, lon_cols)
    returned = behind_lon(behind_lat(dshift))
    grad_in = (grad_out.astype(jnp.float32) + returned.astype(jnp.float32)).astype(jnp.bfloat16)
    total_cells = lax.axis_size("dp") * samples * grid_rows * lon_cols * lax.axis_size(LON)
    factor = float(total_cells) ** (-0.5)
    partial_qkv, partial_proj = (
        scatter_pairs(sums[0], ("lat_0", "lat_1", "lon_0"), "lon_1", 1),
        scatter_pairs(sums[1], ("lat_0", "lat_1", "lon_0"), "lon_1", 1),
    )
    qkv_sum, proj_sum = in_one_piece((partial_qkv, partial_proj), "dp", 0, 1)
    return (grad_in, qkv_sum * factor, proj_sum * factor)


def solution(mesh):
    split = Mesh(
        mesh.devices.reshape(mesh.shape["dp"], 2, 8, 4, 2),
        ("dp", "lat_0", "lat_1", "lon_0", "lon_1"),
    )
    return jax.shard_map(
        per_device,
        mesh=split,
        in_specs=(P("dp", LAT, LON, None), P("dp", LAT, LON, None), P(), P(), P()),
        out_specs=(P("dp", LAT, LON, None), P("dp", LAT_LON), P("dp", LAT_LON)),
        check_vma=False,
    )
```

profile of v0, /device:TPU:1, one launch (start us, length us, event | category | flops | bytes accessed | tf_op | source)
XLA Modules:
  0.0 939.6 jit_solution(12269682326841227891)
XLA Ops:
  14.0 31.3 %collective-permute-done = bf16[2,15,60,384]{3,0,2,1:T(2,128)(2,1)S(1)} collective-permute-done((bf16[2,15,60,384]{3,0,2,1:T(2,128)(2,1)S(1)}, bf16[2,15,60,384]{3,0,2,1:T(2,128)(2,1)S(1)}, u32[]{:S(2)}, u32[]{:S(2)}) %collective-permute-start) | collective-permute-done | bytes 1382432 | tf_op jit(solution)/shard_map/ppermute | solution.py:27
  47.1 3.1 collective-permute-start.1
  52.3 8.0 collective-permute-done.1
  66.9 193.0 %while.33 = (s32[]{:T(128)}, f32[384,1152]{1,0:T(8,128)}, f32[384,384]{1,0:T(8,128)S(1)}, bf16[2,900,384]{2,1,0:T(8,128)(2,1)}, bf16[2,900,384]{2,1,0:T(8,128)(2...) while((s32[]{:T(128)}, f32[384,1152]{1,0:T(8,128)}, ...), condition=%wide.region_9.10_spmd.clone, body=%wide.region_0.9_spmd.clone.sunk | while | flops 3586285568 | bytes 79451888 | solution.py:180
  67.5 2.6 convolution_convert_fusion.8
  75.3 2.7 convolution_convert_fusion.9
  81.0 69.4 %while.34 = (s32[]{:T(128)}, bf16[6,900,64]{1,2,0:T(8,128)(2,1)}, bf16[6,900,64]{1,2,0:T(8,128)(2,1)}, bf16[6,900,64]{1,2,0:T(8,128)(2,1)}, bf16[6,900,64]{1,2,0...) while((s32[]{:T(128)}, bf16[6,900,64]{1,2,0:T(8,128)(2,1)}, ...), condition=%wide.region_6.6_spmd, body=%wide.region_3.5_spmd.sunk | while | flops 640938624 | bytes 29625596 | solution.py:105
  110.8 2.6 fusion.124
  145.4 2.6 fusion.124
  150.5 4.2 fusion.110
  156.6 4.6 convolution_add_fusion.4
  163.6 2.6 convolution_convert_fusion.8
  171.5 2.7 convolution_convert_fusion.9
  177.2 69.4 %while.34 = (s32[]{:T(128)}, bf16[6,900,64]{1,2,0:T(8,128)(2,1)}, bf16[6,900,64]{1,2,0:T(8,128)(2,1)}, bf16[6,900,64]{1,2,0:T(8,128)(2,1)}, bf16[6,900,64]{1,2,0...) while((s32[]{:T(128)}, bf16[6,900,64]{1,2,0:T(8,128)(2,1)}, ...), condition=%wide.region_6.6_spmd, body=%wide.region_3.5_spmd.sunk | while | flops 640938624 | bytes 29625596 | solution.py:105
  206.9 2.6 fusion.124
  241.6 2.6 fusion.124
  246.6 4.2 fusion.110
  252.7 5.2 convolution_add_fusion.4
  270.6 25.2 %all-reduce.7.cloned.1.call-done = f32[128,384,3]{1,2,0:T(4,128)} async-done(((f32[128,384,3]{1,2,0:T(4,128)}), f32[128,384,3]{1,2,0:T(4,128)}) %all-reduce.7.cloned.1.call-update) | async-done | bytes 589840
  297.6 16.4 %reduce-scatter.6.cloned.1.call-done = f32[64,384,9]{1,0,2:T(8,128)} async-done(((f32[128,384,9]{1,0,2:T(8,128)}), f32[64,384,9]{1,0,2:T(8,128)}) %reduce-scatter.6.cloned.1.call-update) | async-done | bytes 884752 | tf_op jit(solution)/shard_map/reduce_scatter | solution.py:41
  315.8 3.3 collective-permute-start.2
  319.0 15.4 %collective-permute-done.2 = bf16[1,15,60,384]{3,1,2,0:T(8,128)(2,1)S(1)} collective-permute-done((bf16[1,15,60,384]{3,1,2,0:T(8,128)(2,1)S(1)}, bf16[1,15,60,384]{3,1,2,0:T(8,128)(2,1)S(1)}, u32[]{:S(2)}, u32[]{:S(2)}) %collective-permute-start.2) | collective-permute-done | bytes 691232 | tf_op jit(solution)/shard_map/ppermute | solution.py:27
  337.5 532.1 %all-reduce.9.cloned.1.call-done = (f32[64,384,3]{1,2,0:T(4,128)}, f32[64,384,9]{1,0,2:T(8,128)}) async-done(((f32[64,384,3]{1,2,0:T(4,128)}, f32[64,384,9]{1,0,2:T(8,128)}), (f32[64,384,3]{1,2,0:T(4,128)}, f32[64,384,9]{1,0,2:T(8,128)})) %all-reduce.9.cloned.1.call-update) | async-done | bytes 1179664
  877.0 52.8 %reduce-scatter.8.cloned.1.call-done = f32[192,12]{1,0:T(8,128)} async-done(((f32[384,12]{1,0:T(8,128)}), f32[192,12]{1,0:T(8,128)}) %reduce-scatter.8.cloned.1.call-update) | async-done | bytes 9232
  (220 shorter events, 197.5 us)
Async XLA Ops:
  7.2 2.4 copy-start.1
  7.2 288.6 %all-reduce.7.cloned.1.call-start = ((), (), s32[]{:S(2)}) async-start(), calls=%async_computation.4 | async-start | bytes 1572864
  12.7 32.6 %collective-permute-start = (bf16[2,15,60,384]{3,0,2,1:T(2,128)(2,1)S(1)}, bf16[2,15,60,384]{3,0,2,1:T(2,128)(2,1)S(1)}, u32[]{:S(2)}, u32[]{:S(2)}) collective-permute-start(bf16[2,15,60,384]{3,0,2,1:T(2,128)(2,1)S(1)} %copy.73), channel_id=1, source_target_pairs={{8,0},{16,8},{24,16},{32,24},{40,32},{48,40},{56,48},{64,56},{72,6... | collective-permute-start | bytes 4147208 | tf_op jit(solution)/shard_map/ppermute | solution.py:27
  47.1 13.2 %collective-permute-start.1 = (bf16[2,30,15,384]{3,0,2,1:T(2,128)(2,1)}, bf16[2,30,15,384]{3,0,2,1:T(2,128)(2,1)}, u32[]{:S(2)}, u32[]{:S(2)}) collective-permute-start(bf16[2,30,15,384]{3,0,2,1:T(2,128)(2,1)} %copy.75), channel_id=1, source_target_pairs={{0,7},{1,0},{2,1},{3,2},{4,3},{5,4},{6,5},{7,6},{8,15},{9,8},{10,9... | collective-permute-start | bytes 2073608 | tf_op jit(solution)/shard_map/ppermute | solution.py:21
  67.1 3.0 copy-start.7
  67.5 2.6 copy-start.9
  150.5 4.2 copy-start.4
  150.5 4.2 copy-start.8
  150.5 4.2 copy-start.10
  156.6 4.6 copy-start
  163.2 3.0 copy-start.7
  163.6 2.7 copy-start.9
  246.6 4.2 copy-start.4
  246.6 4.2 copy-start.8
  246.6 4.3 copy-start.10
  252.7 5.2 copy-start
  262.1 51.9 %reduce-scatter.6.cloned.1.call-start = ((), (), s32[]{:S(2)}) async-start(), calls=%async_computation.2 | async-start | bytes 2654208 | tf_op jit(solution)/shard_map/reduce_scatter | solution.py:41
  268.7 45.4 %copy-start.6 = (bf16[2,900,384]{2,1,0:T(8,128)(2,1)S(1)}, bf16[2,900,384]{2,1,0:T(8,128)(2,1)}, u32[]{:S(2)}) copy-start(bf16[2,900,384]{2,1,0:T(8,128)(2,1)} %get-tuple-element.558) | copy-start | bytes 4147204
  268.7 600.8 %all-reduce.9.cloned.1.call-start = ((), (), s32[]{:S(2)}) async-start(), calls=%async_computation.5 | async-start | bytes 2555904
  314.0 615.8 %reduce-scatter.8.cloned.1.call-start = ((), (), s32[]{:S(2)}) async-start(), calls=%async_computation.3 | async-start | bytes 294912
  315.4 21.5 %copy-start.13 = (u32[256]{0:T(256)S(1)}, u32[256]{0:T(256)}, u32[]{:S(2)}) copy-start(u32[256]{0:T(256)} %constant.75) | copy-start | bytes 3076
  315.8 557.6 %copy-start.2 = (bf16[1,30,60,384]{3,2,1,0:T(8,128)(2,1)S(1)}, bf16[1,30,60,384]{3,2,1,0:T(8,128)(2,1)}, u32[]{:S(2)}) copy-start(bf16[1,30,60,384]{3,2,1,0:T(8,128)(2,1)} %param.10) | copy-start | bytes 4147204
  315.8 18.7 %collective-permute-start.2 = (bf16[1,15,60,384]{3,1,2,0:T(8,128)(2,1)S(1)}, bf16[1,15,60,384]{3,1,2,0:T(8,128)(2,1)S(1)}, u32[]{:S(2)}, u32[]{:S(2)}) collective-permute-start(bf16[1,15,60,384]{3,1,2,0:T(8,128)(2,1)S(1)} %get-tuple-element.279), channel_id=1, source_target_pairs={{0,8},{8,16},{16,24},{24,32},{32,40},{40,48},{48,56},{56,64},{64,7... | collective-permute-start | bytes 2073608 | tf_op jit(solution)/shard_map/ppermute | solution.py:27
  334.5 538.8 %collective-permute-start.3 = (bf16[1,30,15,384]{3,1,2,0:T(8,128)(2,1)S(1)}, bf16[1,30,15,384]{3,1,2,0:T(8,128)(2,1)}, u32[]{:S(2)}, u32[]{:S(2)}) collective-permute-start(bf16[1,30,15,384]{3,1,2,0:T(8,128)(2,1)S(1)} %pad_maximum_fusion.6), channel_id=1, source_target_pairs={{0,1},{1,2},{2,3},{3,4},{4,5},{5,6},{6,7},{7,0},{8,9},{9,10},{10,1... | collective-permute-start | bytes 1036808 | tf_op jit(solution)/shard_map/ppermute | solution.py:21
  (7 other events, 10.1 us)
Sparse Core Ops, SparseCore 0:
  262.2 33.5 all-reduce.6
  298.3 15.6 reduce-scatter.5
  316.7 552.7 all-reduce.8
  873.4 56.3 reduce-scatter.7
where the time goes:
time: 941 us; the launch traced here: 940 us
  waiting for transfers between devices  681 us (72%)
  matrix products  158 us (17%)
  local copies, waits for them, and re-layouts  54.5 us (6%)
  other arithmetic  20.4 us (2%)
  between operations  14.7 us (2%)
  starting transfers between devices  10.1 us (1%)
    unnamed x7, waiting for transfers between devices  610 us
    ppermute x2, waiting for transfers between devices, passed_along(): return lax.ppermute(x, axis, pairs)  46.7 us
    dot_general x12, matrix products, attend_head(): jnp.dot(attention_low.T, grad_rows, preferred_element_type=jnp.float32)  31 us
    dot_general x12, matrix products, attend_head(): jnp.dot(attention_low, value_rows, preferred_element_type=jnp.float32)  29.1 us
    dot_general x12, matrix products, attend_head(): jnp.dot(grad_rows, value_rows.T, preferred_element_type=jnp.float32)  24.9 us
  transfers between devices with their start and end apart: 8, of which 7 were waited for; matrix products, arithmetic and copies ran while one was open for 2% of the time, Pallas kernels for 0%

commit v1 on v0

v1 whole, which is shorter than its diff:
```python
import functools
import jax, jax.numpy as jnp
from jax import lax
from jax.experimental import pallas as pl
from jax.experimental.pallas import tpu as pltpu
from jax.sharding import Mesh
from jax.sharding import PartitionSpec as P
HEADS=6; D=384; HD=64; EPS=1e-5
KC=960; QC=1024; QT=256
BF=bf=jnp.bfloat16
F32=f32=jnp.float32
MESH=pl.DeviceIdType.MESH
NN=(((1,),(0,)),((),())); NT=(((1,),(1,)),((),()))
def dot(a,b,dims=NN): return lax.dot_general(a,b,dims,preferred_element_type=f32)

def window_kernel(group, flag_ref, x_ref, g_ref, gain_ref, wqkv_ref, wqkvT_ref, wp_ref,
                  d_ref, gq_ref, gp_ref,
                  normed, rstd_s, nl, gs, qTa, bTa, kaug, vaug, qkvT, P32, PT, DST, dqkvT, attT):
    gain=gain_ref[...]
    CH=128
    def ln(i,c):
        rows=pl.ds(pl.multiple_of(i*CH,CH),CH)
        x=x_ref[rows,:].astype(f32)
        mu=jnp.sum(x,axis=1,keepdims=True)*(1/D)
        xc=x-mu
        var=jnp.sum(xc*xc,axis=1,keepdims=True)*(1/D)
        rs=lax.rsqrt(var+EPS)
        n=xc*rs
        normed[rows,:]=n
        rstd_s[rows,:]=jnp.broadcast_to(rs,(CH,128))
        nl[rows,:]=(n*gain).astype(bf)
        return c
    lax.fori_loop(0,QC//CH,ln,0)
    zero=jnp.zeros((64,QC),bf)
    for h in range(HEADS):
        o=(h%2)*64
        qh=dot(wqkvT_ref[h*64:(h+1)*64,:],nl[...],NT).astype(bf)
        qkvT[h]=qh
        qTa[h,o:o+64,:]=qh
        qTa[h,64-o:128-o,:]=zero
        bh=dot(wp_ref[h*64:(h+1)*64,:],g_ref[...],NT).astype(bf)
        bTa[h,o:o+64,:]=bh
        bTa[h,64-o:128-o,:]=zero
        one=(lax.broadcasted_iota(jnp.int32,(128,QC),0)==0).astype(f32).astype(bf)
        qTa[h,128:256,:]=one
        bTa[h,128:256,:]=jnp.zeros((128,QC),bf)
    for h in range(HEADS,3*HEADS):
        qkvT[h]=dot(wqkvT_ref[h*64:(h+1)*64,:],nl[...],NT).astype(bf)
    row=lax.broadcasted_iota(jnp.int32,(KC,128),0)
    lane=lax.broadcasted_iota(jnp.int32,(KC,128),1)
    bad=(lax.rem(row,group)>=group-group//15)|((row>=KC//2)&(flag_ref[0]==0))
    bias=jnp.where((lane==0)&bad,-30000.0,0.0).astype(bf)
    ones=jnp.where(lane<2,1.0,0.0).astype(bf)
    for j in range(3):
        kaug[j,:,0:128]=dot(nl[0:KC,:],wqkv_ref[:,D+j*128:D+(j+1)*128]).astype(bf)
        vaug[j,:,0:128]=dot(nl[0:KC,:],wqkv_ref[:,2*D+j*128:2*D+(j+1)*128]).astype(bf)
        kaug[j,:,128:256]=bias
        vaug[j,:,128:256]=ones
    CK=240
    def head(h,c):
        j=h//2
        o=pl.multiple_of((h%2)*64,64)
        for t in range(QC//QT):
            ts=slice(t*QT,(t+1)*QT)
            acc=jnp.zeros((8,QT),f32)
            for k in range(0,KC,CK):
                e=jnp.exp(dot(kaug[j,k:k+CK,:],qTa[h,:,ts]))
                P32[k:k+CK,ts]=e
                acc=acc+jnp.sum(e.reshape(CK//8,8,QT),axis=0)
            r=1.0/jnp.sum(acc,axis=0,keepdims=True)
            for k in range(0,KC,CK):
                p=P32[k:k+CK,ts]*r
                P32[k:k+CK,ts]=p
                PT[k:k+CK,ts]=p.astype(bf)
            a=dot(qkvT[12+h][:,0:KC],PT[:,ts])
            attT[h,:,ts]=a.astype(bf)
            nd=-jnp.sum(a*bTa[h,pl.ds(o,64),ts].astype(f32),axis=0,keepdims=True)
            hi=nd.astype(bf).astype(f32)
            lo=nd-hi
            r16=lax.broadcasted_iota(jnp.int32,(16,QT),0)
            bTa[h,128:144,ts]=jnp.where(r16==0,hi,jnp.where(r16==1,lo,0.0)).astype(bf)
            for k in range(0,KC,CK):
                dp=dot(vaug[j,k:k+CK,:],bTa[h,:,ts])
                DST[k:k+CK,ts]=(P32[k:k+CK,ts]*dp).astype(bf)
            dqkvT[h,:,ts]=dot(qkvT[6+h][:,0:KC],DST[:,ts]).astype(bf)
        dqkvT[6+h,:,0:KC]=dot(qkvT[h],DST[...],NT).astype(bf)
        dqkvT[12+h,:,0:KC]=dot(bTa[h,pl.ds(o,64),:],PT[...],NT).astype(bf)
        return c
    dqkvT[:,:,KC:]=jnp.zeros((18,64,QC-KC),bf)
    lax.fori_loop(0,HEADS,head,0)
    dall=dqkvT[...].reshape(3*D,QC)
    gq_ref[...]=dot(dall,nl[...])
    gp_ref[...]=dot(attT[...].reshape(D,QC),g_ref[...])
    for t in range(QC//QT):
        rows=slice(t*QT,(t+1)*QT)
        dn=dot(wqkv_ref[...],dqkvT[:,:,rows].reshape(3*D,QT)).T*gain
        n=normed[rows,:]
        m1=jnp.sum(dn,axis=1,keepdims=True)*(1/D)
        m2=jnp.sum(dn*n,axis=1,keepdims=True)*(1/D)
        d_ref[rows,:]=(rstd_s[rows,0:1]*(dn-m1-n*m2)).astype(bf)

def window_call(group, flag, x, g, gain, wqkv, wqkvT, wp):
    V=pl.BlockSpec(memory_space=pltpu.VMEM)
    return pl.pallas_call(
        functools.partial(window_kernel,group),
        out_shape=(jax.ShapeDtypeStruct((QC,D),bf),jax.ShapeDtypeStruct((3*D,D),f32),jax.ShapeDtypeStruct((D,D),f32)),
        in_specs=[pl.BlockSpec(memory_space=pltpu.SMEM)]+[V]*6,
        out_specs=(V,V,V),
        scratch_shapes=[pltpu.VMEM(s,d) for s,d in [((QC,D),f32),((QC,128),f32),((QC,D),bf),((8,128),bf),
            ((6,256,QC),bf),((6,256,QC),bf),((3,KC,256),bf),((3,KC,256),bf),((18,64,QC),bf),
            ((KC,QC),f32),((KC,QC),bf),((KC,QC),bf),((18,64,QC),bf),((6,64,QC),bf)]],
        compiler_params=pltpu.CompilerParams(vmem_limit_bytes=60*1024*1024),
        cost_estimate=pl.CostEstimate(flops=8*10**9,bytes_accessed=10**7,transcendentals=6*10**6),
        name="window_grads",
    )(flag, x, g, gain, wqkv, wqkvT, wp)


def reduce_kernel(gqa, gqb, gpa, gpb, out, total, core_send, core_recv, core_own, y_send, y_recv, y_own,
                  lat_send, lat_recv, dp_send, dp_recv, send_sems, recv_sems):
    xl, z, y, core = (lax.axis_index(n) for n in ("xl", "z", "y", "core"))
    dp = lax.axis_index("dp")
    lat = xl * 8 + z

    def lat_peer(k):
        t = lax.rem(lat + k, 16)
        return t, {"xl": t // 8, "z": lax.rem(t, 8)}

    barrier = pltpu.get_barrier_semaphore()
    peers = [{"core": 1 - core}, {"dp": 1 - dp}]
    peers += [{"y": lax.rem(y + k, 4)} for k in range(1, 4)]
    peers += [lat_peer(k)[1] for k in range(1, 16)]
    for peer in peers:
        pl.semaphore_signal(barrier, inc=1, device_id=peer, device_id_type=MESH)

    for n in range(3):
        total[n, 0:1152, :] = gqa[:, n * 128:(n + 1) * 128] + gqb[:, n * 128:(n + 1) * 128]
        rows = slice(n * 128, (n + 1) * 128)
        total[n, 1152:1536, :] = (gpa[rows, :] + gpb[rows, :]).T

    def gather(lon, j):
        first, step = (9 * lon + j, 72) if j < 9 else (1152 + 3 * lon + j - 9, 24)
        return jnp.concatenate([total[n, pl.ds(first, 16, stride=step), :] for n in range(3)], axis=1)

    def strided(ref, first):
        return jnp.concatenate([ref[n, pl.ds(first, 12, stride=16), :] for n in range(3)], axis=1)

    def copy(src, dst, number, peer):
        return pltpu.make_async_remote_copy(
            src_ref=src, dst_ref=dst, send_sem=send_sems.at[number], recv_sem=recv_sems.at[number],
            device_id=peer, device_id_type=MESH)

    core_copies = []
    for i in range(4):
        for j in range(12):
            core_send[i, j * 16:(j + 1) * 16, :] = gather(2 * i + 1 - core, j).astype(BF)
        if i == 0:
            pl.semaphore_wait(barrier, len(peers))
        c = copy(core_send.at[i], core_recv.at[i], i, {"core": 1 - core})
        c.start()
        core_copies.append(c)
    for i in range(4):
        for j in range(12):
            core_own[i, j * 16:(j + 1) * 16, :] = gather(2 * i + core, j)
    for i in range(4):
        core_copies[i].wait()
        core_own[i] = core_own[i] + core_recv[i].astype(F32)
    y_copies = []
    for k in range(1, 4):
        t = lax.rem(y + k, 4)
        y_send[k - 1] = core_own[t].astype(BF)
        c = copy(y_send.at[k - 1], y_recv.at[k - 1], 3 + k, {"y": t})
        c.start()
        y_copies.append(c)
    for k in range(3):
        y_copies[k].wait()
    mine = core_own[y] + y_recv[0].astype(F32) + y_recv[1].astype(F32) + y_recv[2].astype(F32)
    for n in range(3):
        y_own[n] = mine[:, n * 128:(n + 1) * 128]
    lat_send[...] = jnp.zeros_like(lat_send)
    for t in range(16):
        lat_send[t, 0:12, :] = strided(y_own, t).astype(BF)
    lat_copies = []
    for k in range(1, 16):
        t, peer = lat_peer(k)
        c = copy(lat_send.at[t], lat_recv.at[k - 1], 6 + k, peer)
        c.start()
        lat_copies.append(c)
    own = strided(y_own, lat)
    for k in range(15):
        lat_copies[k].wait()
        own = own + lat_recv[k, 0:12, :].astype(F32)
    dp_send[...] = jnp.zeros_like(dp_send)
    dp_send[0:12, :] = own
    c = copy(dp_send, dp_recv, 22, {"dp": 1 - dp})
    c.start()
    c.wait()
    out[...] = dp_send[...] + dp_recv[...]


def reduce_call(gqa, gqb, gpa, gpb):
    V = pl.BlockSpec(memory_space=pltpu.VMEM)
    return pl.pallas_call(
        reduce_kernel,
        out_shape=jax.ShapeDtypeStruct((16, D), F32),
        in_specs=[V] * 4,
        out_specs=V,
        scratch_shapes=[
            pltpu.VMEM((3, 1536, 128), F32),
            pltpu.VMEM((4, 192, D), BF),
            pltpu.VMEM((4, 192, D), BF),
            pltpu.VMEM((4, 192, D), F32),
            pltpu.VMEM((3, 192, D), BF),
            pltpu.VMEM((3, 192, D), BF),
            pltpu.VMEM((3, 192, 128), F32),
            pltpu.VMEM((16, 16, D), BF),
            pltpu.VMEM((15, 16, D), BF),
            pltpu.VMEM((16, D), F32),
            pltpu.VMEM((16, D), F32),
            pltpu.SemaphoreType.DMA((23,)),
            pltpu.SemaphoreType.DMA((23,)),
        ],
        compiler_params=pltpu.CompilerParams(
            vmem_limit_bytes=40 * 1024 * 1024, collective_id=0, has_side_effects=True),
        name="reduce_grads",
    )(gqa, gqb, gpa, gpb)


LAT = ("xl", "z")
LON = ("y", "core")
BOTH = LAT + LON


def moved(value, lat_by, lon_by, wrap):
    pairs = []
    for r in range(16):
        for c in range(8):
            if not wrap and not 0 <= r + lat_by < 16:
                continue
            pairs.append((r * 8 + c, (r + lat_by) % 16 * 8 + (c + lon_by) % 8))
    return lax.ppermute(value, BOTH, pairs)


def padded(value, to):
    return jnp.pad(value, ((0, 0), (0, 0), (0, to - value.shape[2]), (0, 0)))


def rows_of(value):
    return value.reshape(2, KC, D)


def per_device(hidden_in, grad_out, norm_gain, w_qkv, w_proj):
    r = lax.axis_index(LAT)
    both = jnp.concatenate([hidden_in, grad_out], axis=0)
    top, bottom = both[:, :15], both[:, 15:]
    a_in = moved(top[:, :, 15:45], -1, 0, False)
    b_br = moved(bottom[:, :, 45:], 1, 0, True)
    b_tl = moved(top[:, :, :15], 0, -1, True)
    b_bl = moved(bottom[:, :, :15], 1, -1, True)

    scale = jnp.where(jnp.arange(3 * D) < D, 0.125, 1.0).astype(F32)
    wqkv = (w_qkv.astype(F32) * scale).astype(BF)
    wqkv_t = wqkv.T
    gain = norm_gain.reshape(1, D)

    win_a = padded(jnp.concatenate([bottom[:, :, 15:45], a_in], axis=1), 32).reshape(2, KC, D)
    flag_a = (r < 15).astype(jnp.int32).reshape(1)
    inside = (r > 0).astype(jnp.int32).reshape(1)
    lower = jnp.concatenate([padded(b_br, 16), padded(b_bl, 16)], axis=2)
    upper = jnp.concatenate([padded(top[:, :, 45:], 16), padded(b_tl, 16)], axis=2)
    upper = jnp.where(r > 0, upper, jnp.zeros_like(upper))
    win_b = jnp.concatenate([lower, upper], axis=1).reshape(2, KC, D)
    win_a = jnp.pad(win_a, ((0, 0), (0, QC - KC), (0, 0)))
    win_b = jnp.pad(win_b, ((0, 0), (0, QC - KC), (0, 0)))

    da, gqa, gpa = window_call(32, flag_a, win_a[0], win_a[1], gain, wqkv, wqkv_t, w_proj)
    db, gqb, gpb = window_call(16, inside, win_b[0], win_b[1], gain, wqkv, wqkv_t, w_proj)

    da = da[:KC].reshape(1, 30, 32, D)
    db = db[:KC].reshape(1, 30, 32, D)
    t_m = moved(da[:, 15:, :30], 1, 0, False)
    b_r = moved(db[:, :15, :15], -1, 0, True)
    t_l = moved(db[:, 15:, 16:31], 0, 1, True)
    b_l = moved(db[:, :15, 16:31], -1, 1, True)
    back = jnp.concatenate([
        jnp.concatenate([t_l, t_m, db[:, 15:, :15]], axis=2),
        jnp.concatenate([b_l, da[:, :15, :30], b_r], axis=2)], axis=1)
    grad_in = (grad_out.astype(F32) + back.astype(F32)).astype(BF)

    sums = reduce_call(gqa, gqb, gpa, gpb)
    mine = lax.dynamic_slice_in_dim(sums, lax.axis_index("dp") * 192, 192, axis=1)[:12].T
    first = lax.axis_index(BOTH) * 9
    factor = 460800.0 ** -0.5
    column = jnp.where(first + jnp.arange(9) < D, 0.125 * factor, factor)
    return grad_in, mine[:, :9] * column[None, :], mine[:, 9:] * factor


def solution(mesh):
    split = Mesh(mesh.devices.reshape(2, 2, 8, 4, 2), ("dp", "xl", "z", "y", "core"))
    return jax.shard_map(
        per_device,
        mesh=split,
        in_specs=(P("dp", LAT, LON, None), P("dp", LAT, LON, None), P(), P(), P()),
        out_specs=(P("dp", LAT, LON, None), P("dp", BOTH), P("dp", BOTH)),
        check_vma=False,
    )
```

time: 941 us -> 163 us (0.17)
  waiting for transfers between devices: 681 us -> 7.73 us
  matrix products: 158 us -> 0 us
  Pallas kernels: 0 us -> 113 us
  local copies, waits for them, and re-layouts: 54.5 us -> 15.2 us
  between operations: 14.7 us -> 0.82 us
  other arithmetic: 20.4 us -> 8.27 us
    unnamed x7 -> x0, waiting for transfers between devices: 610 us -> none
    dot_general x82 -> x0, matrix products: 158 us -> none  [the longest x12 31 us: attend_head(): jnp.dot(attention_low.T, grad_rows, preferred_element_type=jnp.float32)]
    pallas_call x0 -> x3, Pallas kernels: none -> 113 us  [the longest x2 87.9 us: window_call(): pl.pallas_call(functools.partial(window_kernel, group), out_shape=(jax.Sh...]
    ppermute x4 -> x8, waiting for transfers between devices: 54.7 us -> 7.73 us  [moved(): return lax.ppermute(value, BOTH, pairs)]
    reduce_scatter x1 -> x0, waiting for transfers between devices: 16.4 us -> none  [scatter_pairs(): pieces = lax.psum_scatter(pieces, core, scatter_dimension=0, tiled=True)]
    convert_element_type x14 -> x2, other arithmetic: 15.1 us -> 2.09 us  [the longest x1 1.87 us: per_device(): grad_in = (grad_out.astype(F32) + back.astype(F32)).astype(BF)]
    slice x13 -> x6, local copies, waits for them, and re-layouts: 15.4 us -> 5.97 us  [the longest x1 1.93 us: per_device(): bottom[:, :, 15:45]]
  transfers between devices with their start and end apart: 8 -> 8, of which waited for: 7 -> 2; matrix products, arithmetic and copies ran while one was open for 2% -> 10% of each run, Pallas kernels for 0% -> 70%
where the time goes in v1:
time: 163 us; the launch traced here: 162 us
  Pallas kernels  113 us (69%)
  starting transfers between devices  16.7 us (10%)
  local copies, waits for them, and re-layouts  15.2 us (9%)
  other arithmetic  8.27 us (5%)
  waiting for transfers between devices  7.73 us (5%)
    pallas_call x2, Pallas kernels, window_call(): pl.pallas_call(functools.partial(window_kernel, group), out_shape=(jax.Sh...  87.9 us
    pallas_call x1, Pallas kernels, reduce_call(): pl.pallas_call(reduce_kernel, out_shape=jax.ShapeDtypeStruct((16, D), F32...  25.6 us
    ppermute x8, starting transfers between devices, moved(): return lax.ppermute(value, BOTH, pairs)  16.7 us
    ppermute x8, waiting for transfers between devices, moved(): return lax.ppermute(value, BOTH, pairs)  7.73 us
    unnamed x20, local copies, waits for them, and re-layouts  4.17 us
  transfers between devices with their start and end apart: 8, of which 2 were waited for; matrix products, arithmetic and copies ran while one was open for 10% of the time, Pallas kernels for 70%

profile of v1, /device:TPU:1, one launch (start us, length us, event | category | flops | bytes accessed | tf_op | source)
XLA Modules:
  0.0 162.1 jit_solution(1822731935812231172)
XLA Ops:
  0.6 1.6 %constant_dynamic-update-slice_fusion.1 = bf16[2,30,60,384]{3,2,1,0:T(8,128)(2,1)S(1)} fusion(bf16[1,30,60,384]{3,2,1,0:T(8,128)(2,1)} %param.5), kind=kLoop, calls=%fused_computation.36 | loop fusion | bytes 2856960
  2.8 1.3 fusion.21
  4.0 3.0 %collective-permute-start.1 = (bf16[2,15,15,384]{3,2,1,0:T(8,128)(2,1)}, bf16[2,15,15,384]{3,2,1,0:T(8,128)(2,1)}, u32[]{:S(2)}, u32[]{:S(2)}) collective-permute-start(bf16[2,15,15,384]{3,2,1,0:T(8,128)(2,1)} %get-tuple-element.19), channel_id=1, source_target_pairs={{0,15},{1,8},{2,9},{3,10},{4,11},{5,12},{6,13},{7,14},{8,23},{9,16... | collective-permute-start | bytes 1036808 | tf_op jit(solution)/shard_map/ppermute | solution.py:240
  7.1 1.6 %collective-permute-start = (bf16[2,15,15,384]{3,2,1,0:T(8,128)(2,1)}, bf16[2,15,15,384]{3,2,1,0:T(8,128)(2,1)}, u32[]{:S(2)}, u32[]{:S(2)}) collective-permute-start(bf16[2,15,15,384]{3,2,1,0:T(8,128)(2,1)} %get-tuple-element.20), channel_id=1, source_target_pairs={{0,8},{1,9},{2,10},{3,11},{4,12},{5,13},{6,14},{7,15},{8,16},{9,17... | collective-permute-start | bytes 1036808 | tf_op jit(solution)/shard_map/ppermute | solution.py:240
  8.7 2.6 %collective-permute-start.2 = (bf16[2,15,15,384]{3,2,1,0:T(8,128)(2,1)}, bf16[2,15,15,384]{3,2,1,0:T(8,128)(2,1)}, u32[]{:S(2)}, u32[]{:S(2)}) collective-permute-start(bf16[2,15,15,384]{3,2,1,0:T(8,128)(2,1)} %get-tuple-element.18), channel_id=1, source_target_pairs={{0,7},{1,0},{2,1},{3,2},{4,3},{5,4},{6,5},{7,6},{8,15},{9,8},{10,9... | collective-permute-start | bytes 1036808 | tf_op jit(solution)/shard_map/ppermute | solution.py:240
  11.3 1.9 %fusion.20 = (bf16[2,15,30,384]{3,2,1,0:T(8,128)(2,1)}, bf16[2,15,30,384]{3,2,1,0:T(8,128)(2,1)}) fusion(bf16[2,30,60,384]{3,2,1,0:T(8,128)(2,1)S(1)} %constant_dynamic-update-slice_fusion), kind=kLoop, calls=%fused_computation.39 | loop fusion | bytes 2764800 | tf_op jit(solution)/shard_map/slice | solution.py:265
  13.2 1.5 collective-permute-start.4
  17.5 1.5 copy.9.wqkv_ref
  19.0 1.2 fusion.18
  20.2 2.2 %collective-permute-done.1 = bf16[2,15,15,384]{3,2,1,0:T(8,128)(2,1)} collective-permute-done((bf16[2,15,15,384]{3,2,1,0:T(8,128)(2,1)}, bf16[2,15,15,384]{3,2,1,0:T(8,128)(2,1)}, u32[]{:S(2)}, u32[]{:S(2)}) %collective-permute-start.1) | collective-permute-done | bytes 345632 | tf_op jit(solution)/shard_map/ppermute | solution.py:240
  22.4 5.5 %collective-permute-done = bf16[2,15,15,384]{3,2,1,0:T(8,128)(2,1)} collective-permute-done((bf16[2,15,15,384]{3,2,1,0:T(8,128)(2,1)}, bf16[2,15,15,384]{3,2,1,0:T(8,128)(2,1)}, u32[]{:S(2)}, u32[]{:S(2)}) %collective-permute-start) | collective-permute-done | bytes 345632 | tf_op jit(solution)/shard_map/ppermute | solution.py:240
  27.9 1.3 fusion.9
  29.2 1.3 fusion.14
  30.5 44.1 %window_grads.2 = (bf16[1024,384]{1,0:T(8,128)(2,1)}, f32[1152,384]{1,0:T(8,128)}, f32[384,384]{1,0:T(8,128)}) custom-call(s32[1]{0:T(128)} %bitcast.flag_ref, bf16[1024,384]{1,0:T(8,128)(2,1)} %get-tuple-element.24.x_ref, bf16[1024,384]{1,0:T(8,128)(2,1)} %get-tuple-element.23.g_ref, f32[1,384]{1,0:T(1,128)} %reshape.73.gain_ref, ...), custom_call_target="tpu_custom_call" | custom-call | flops 8000000000 | bytes 10000000 | tf_op jit(solution)/shard_map/window_grads/pallas_call | solution.py:104
  74.5 1.3 slice.77
  76.4 4.6 %collective-permute-start.6 = (bf16[1,15,15,384]{3,2,1,0:T(8,128)(2,1)S(1)}, bf16[1,15,15,384]{3,2,1,0:T(8,128)(2,1)S(1)}, u32[]{:S(2)}, u32[]{:S(2)}) collective-permute-start(bf16[1,15,15,384]{3,2,1,0:T(8,128)(2,1)S(1)} %get-tuple-element.27), channel_id=1, source_target_pairs={{0,121},{1,122},{2,123},{3,124},{4,125},{5,126},{6,127},{7,120},{8... | collective-permute-start | bytes 518408 | tf_op jit(solution)/shard_map/ppermute | solution.py:240
  81.1 1.3 fusion.10
  82.4 1.3 fusion.16
  83.7 43.8 %window_grads.3 = (bf16[1024,384]{1,0:T(8,128)(2,1)}, f32[1152,384]{1,0:T(8,128)}, f32[384,384]{1,0:T(8,128)}) custom-call(s32[1]{0:T(128)} %bitcast.6.flag_ref, bf16[1024,384]{1,0:T(8,128)(2,1)} %get-tuple-element.22.x_ref, bf16[1024,384]{1,0:T(8,128)(2,1)} %get-tuple-element.21.g_ref, f32[1,384]{1,0:T(1,128)} %reshape.73.gain_ref, ...), custom_call_target="tpu_custom_call" | custom-call | flops 8000000000 | bytes 10000000 | tf_op jit(solution)/shard_map/window_grads/pallas_call | solution.py:104
  127.5 1.3 slice.83
  128.9 2.8 %collective-permute-start.5 = (bf16[1,15,30,384]{3,2,1,0:T(8,128)(2,1)S(1)}, bf16[1,15,30,384]{3,2,1,0:T(8,128)(2,1)S(1)}, u32[]{:S(2)}, u32[]{:S(2)}) collective-permute-start(bf16[1,15,30,384]{3,2,1,0:T(8,128)(2,1)S(1)} %get-tuple-element.29), channel_id=1, source_target_pairs={{0,8},{1,9},{2,10},{3,11},{4,12},{5,13},{6,14},{7,15},{8,16},{9,17... | collective-permute-start | bytes 1036808 | tf_op jit(solution)/shard_map/ppermute | solution.py:240
  131.8 1.5 copy-done.1
  133.3 25.6 %reduce_grads.1 = f32[16,384]{1,0:T(8,128)S(1)} custom-call(f32[1152,384]{1,0:T(8,128)S(1)} %copy-done.1, f32[1152,384]{1,0:T(8,128)S(1)} %copy-done, f32[384,384]{1,0:T(8,128)S(1)} %copy-done.3, f32[384,384]{1,0:T(8,128)S(1)} %copy-done.2), custom_call_target="tpu_custom_call" | custom-call | tf_op jit(solution)/shard_map/reduce_grads/pallas_call | solution.py:202
  160.2 1.9 %add_convert_fusion = bf16[1,30,60,384]{3,2,1,0:T(8,128)(2,1)} fusion(bf16[1,30,60,384]{3,2,1,0:T(8,128)(2,1)S(1)} %copy-done.4, bf16[1,15,15,384]{3,2,1,0:T(8,128)(2,1)S(1)} %collective-permute-done.7, bf16[1,15,30,384]{3,2,1,0:T(8,128)(2,1)S(1)} %get-tuple-element.30, bf16[1,15,15,384]{3,2,1,0:T(8,128)(2,1)S(1)} %collective-permute-done.6, ...), kind=kLoop, calls=%fused_computation.10 | loop fusion | flops 10368000 | bytes 4147200 | tf_op jit(solution)/shard_map/convert_element_type | solution.py:287
  (37 shorter events, 5.4 us)
Async XLA Ops:
  0.6 1.8 %copy-start.4 = (bf16[1,30,60,384]{3,2,1,0:T(8,128)(2,1)S(1)}, bf16[1,30,60,384]{3,2,1,0:T(8,128)(2,1)}, u32[]{:S(2)}) copy-start(bf16[1,30,60,384]{3,2,1,0:T(8,128)(2,1)} %param.6) | copy-start | bytes 4147204
  4.0 10.6 %copy-start.7 = (bf16[384,1152]{1,0:T(8,128)(2,1)S(1)}, bf16[384,1152]{1,0:T(8,128)(2,1)}, u32[]{:S(2)}) copy-start(bf16[384,1152]{1,0:T(8,128)(2,1)} %param.8) | copy-start | bytes 2654212
  4.0 18.4 %collective-permute-start.1 = (bf16[2,15,15,384]{3,2,1,0:T(8,128)(2,1)}, bf16[2,15,15,384]{3,2,1,0:T(8,128)(2,1)}, u32[]{:S(2)}, u32[]{:S(2)}) collective-permute-start(bf16[2,15,15,384]{3,2,1,0:T(8,128)(2,1)} %get-tuple-element.19), channel_id=1, source_target_pairs={{0,15},{1,8},{2,9},{3,10},{4,11},{5,12},{6,13},{7,14},{8,23},{9,16... | collective-permute-start | bytes 1036808 | tf_op jit(solution)/shard_map/ppermute | solution.py:240
  7.1 20.8 %collective-permute-start = (bf16[2,15,15,384]{3,2,1,0:T(8,128)(2,1)}, bf16[2,15,15,384]{3,2,1,0:T(8,128)(2,1)}, u32[]{:S(2)}, u32[]{:S(2)}) collective-permute-start(bf16[2,15,15,384]{3,2,1,0:T(8,128)(2,1)} %get-tuple-element.20), channel_id=1, source_target_pairs={{0,8},{1,9},{2,10},{3,11},{4,12},{5,13},{6,14},{7,15},{8,16},{9,17... | collective-permute-start | bytes 1036808 | tf_op jit(solution)/shard_map/ppermute | solution.py:240
  8.7 10.3 %collective-permute-start.2 = (bf16[2,15,15,384]{3,2,1,0:T(8,128)(2,1)}, bf16[2,15,15,384]{3,2,1,0:T(8,128)(2,1)}, u32[]{:S(2)}, u32[]{:S(2)}) collective-permute-start(bf16[2,15,15,384]{3,2,1,0:T(8,128)(2,1)} %get-tuple-element.18), channel_id=1, source_target_pairs={{0,7},{1,0},{2,1},{3,2},{4,3},{5,4},{6,5},{7,6},{8,15},{9,8},{10,9... | collective-permute-start | bytes 1036808 | tf_op jit(solution)/shard_map/ppermute | solution.py:240
  13.2 67.9 %collective-permute-start.4 = (bf16[2,15,30,384]{3,2,1,0:T(8,128)(2,1)}, bf16[2,15,30,384]{3,2,1,0:T(8,128)(2,1)}, u32[]{:S(2)}, u32[]{:S(2)}) collective-permute-start(bf16[2,15,30,384]{3,2,1,0:T(8,128)(2,1)} %get-tuple-element.16), channel_id=1, source_target_pairs={{8,0},{9,1},{10,2},{11,3},{12,4},{13,5},{14,6},{15,7},{16,8},{17,9... | collective-permute-start | bytes 2073608 | tf_op jit(solution)/shard_map/ppermute | solution.py:240
  15.6 1.4 copy-start.8
  16.9 2.1 %copy-start.6 = (bf16[2,15,15,384]{3,2,1,0:T(8,128)(2,1)S(1)}, bf16[2,15,15,384]{3,2,1,0:T(8,128)(2,1)}, u32[]{:S(2)}) copy-start(bf16[2,15,15,384]{3,2,1,0:T(8,128)(2,1)} %get-tuple-element.17) | copy-start | bytes 1036804
  74.5 6.5 %copy-start.5 = (bf16[2,15,30,384]{3,2,1,0:T(8,128)(2,1)S(1)}, bf16[2,15,30,384]{3,2,1,0:T(8,128)(2,1)}, u32[]{:S(2)}) copy-start(bf16[2,15,30,384]{3,2,1,0:T(8,128)(2,1)} %get-tuple-element.15) | copy-start | bytes 2073604
  75.9 84.3 %collective-permute-start.7 = (bf16[1,15,15,384]{3,2,1,0:T(8,128)(2,1)S(1)}, bf16[1,15,15,384]{3,2,1,0:T(8,128)(2,1)S(1)}, u32[]{:S(2)}, u32[]{:S(2)}) collective-permute-start(bf16[1,15,15,384]{3,2,1,0:T(8,128)(2,1)S(1)} %get-tuple-element.26), channel_id=1, source_target_pairs={{0,120},{1,121},{2,122},{3,123},{4,124},{5,125},{6,126},{7,127},{8... | collective-permute-start | bytes 518408 | tf_op jit(solution)/shard_map/ppermute | solution.py:240
  76.4 83.8 %collective-permute-start.6 = (bf16[1,15,15,384]{3,2,1,0:T(8,128)(2,1)S(1)}, bf16[1,15,15,384]{3,2,1,0:T(8,128)(2,1)S(1)}, u32[]{:S(2)}, u32[]{:S(2)}) collective-permute-start(bf16[1,15,15,384]{3,2,1,0:T(8,128)(2,1)S(1)} %get-tuple-element.27), channel_id=1, source_target_pairs={{0,121},{1,122},{2,123},{3,124},{4,125},{5,126},{6,127},{7,120},{8... | collective-permute-start | bytes 518408 | tf_op jit(solution)/shard_map/ppermute | solution.py:240
  80.9 79.3 %collective-permute-start.3 = (bf16[1,15,15,384]{3,2,1,0:T(8,128)(2,1)S(1)}, bf16[1,15,15,384]{3,2,1,0:T(8,128)(2,1)S(1)}, u32[]{:S(2)}, u32[]{:S(2)}) collective-permute-start(bf16[1,15,15,384]{3,2,1,0:T(8,128)(2,1)S(1)} %get-tuple-element.25), channel_id=1, source_target_pairs={{0,1},{1,2},{2,3},{3,4},{4,5},{5,6},{6,7},{7,0},{8,9},{9,10},{10,1... | collective-permute-start | bytes 518408 | tf_op jit(solution)/shard_map/ppermute | solution.py:240
  127.5 4.3 %copy-start = (f32[1152,384]{1,0:T(8,128)S(1)}, f32[1152,384]{1,0:T(8,128)}, u32[]{:S(2)}) copy-start(f32[1152,384]{1,0:T(8,128)} %get-tuple-element.12.gqb) | copy-start | bytes 5308420
  127.5 4.3 %copy-start.2 = (f32[384,384]{1,0:T(8,128)S(1)}, f32[384,384]{1,0:T(8,128)}, u32[]{:S(2)}) copy-start(f32[384,384]{1,0:T(8,128)} %get-tuple-element.14.gpb) | copy-start | bytes 1769476
  127.5 4.3 %copy-start.3 = (f32[384,384]{1,0:T(8,128)S(1)}, f32[384,384]{1,0:T(8,128)}, u32[]{:S(2)}) copy-start(f32[384,384]{1,0:T(8,128)} %get-tuple-element.13.gpa) | copy-start | bytes 1769476
  128.9 31.3 %collective-permute-start.5 = (bf16[1,15,30,384]{3,2,1,0:T(8,128)(2,1)S(1)}, bf16[1,15,30,384]{3,2,1,0:T(8,128)(2,1)S(1)}, u32[]{:S(2)}, u32[]{:S(2)}) collective-permute-start(bf16[1,15,30,384]{3,2,1,0:T(8,128)(2,1)S(1)} %get-tuple-element.29), channel_id=1, source_target_pairs={{0,8},{1,9},{2,10},{3,11},{4,12},{5,13},{6,14},{7,15},{8,16},{9,17... | collective-permute-start | bytes 1036808 | tf_op jit(solution)/shard_map/ppermute | solution.py:240
  131.8 1.5 copy-start.1

commit v2 on v0

v2 whole, which is shorter than its diff:
```python
import jax
import jax.numpy as jnp
from jax import lax
from jax.experimental import pallas as pl
from jax.experimental.pallas import tpu as pltpu
from jax.sharding import Mesh
from jax.sharding import PartitionSpec as P

HEADS = 6
D = 384
EPS = 1e-5
KC = 960
QC = 1024
CK = 480
BF = jnp.bfloat16
F32 = jnp.float32
MESH = pl.DeviceIdType.MESH
NN = (((1,), (0,)), ((), ()))
NT = (((1,), (1,)), ((), ()))
LAT = ("xl", "z")
LON = ("y", "core")
BOTH = LAT + LON


def dot(a, b, dims=NN):
    return lax.dot_general(a, b, dims, preferred_element_type=F32)


def kernel(x_ref, g_ref, gain_ref, w_ref, wp_ref, out_ref, sums_ref,
           buf, s_a, s_br, s_tl, s_bl, dbuf, ret_tm, ret_br, ret_bl, ret_tl,
           w_t, normed, rstd_s, nl, gs, q_aug, b_aug, k_aug, v_aug, qkv_t, p32, p_low, ds_low, dqkv_t, att_t,
           gp, total, core_send, core_recv, core_own, y_send, y_recv, y_own, lat_send, lat_recv,
           dp_send, dp_recv, send_sems, recv_sems):
    dp, xl, z, y, core = (lax.axis_index(n) for n in ("dp", "xl", "z", "y", "core"))
    lat = xl * 8 + z
    lon = y * 2 + core

    def at(lat_by, lon_by):
        t = lax.rem(lat + lat_by + 16, 16)
        u = lax.rem(lon + lon_by + 8, 8)
        return {"xl": t // 8, "z": lax.rem(t, 8), "y": u // 2, "core": lax.rem(u, 2)}

    def copy(src, dst, number, peer):
        return pltpu.make_async_remote_copy(
            src_ref=src, dst_ref=dst, send_sem=send_sems.at[number], recv_sem=recv_sems.at[number],
            device_id=peer, device_id_type=MESH)

    barrier = pltpu.get_barrier_semaphore()
    partner = {"core": 1 - core}
    peers = [partner, {"dp": 1 - dp}, at(0, -1), at(0, 1), at(1, -1), at(-1, 1)]
    peers += [{"y": lax.rem(y + k, 4)} for k in range(1, 4)]
    peers += [at(k, 0) for k in range(1, 16)]
    for peer in peers:
        pl.semaphore_signal(barrier, inc=1, device_id=peer, device_id_type=MESH)

    halo_a = copy(s_a, buf.at[0, :, 15:30], 23, at(-1, 0))
    halo_br = copy(s_br, buf.at[1, :, 0:15, 0:16], 24, at(1, 0))
    halo_tl = copy(s_tl, buf.at[1, :, 15:30, 16:32], 25, at(0, -1))
    halo_bl = copy(s_bl, buf.at[1, :, 0:15, 16:32], 26, at(1, -1))
    back_tm = copy(dbuf.at[0, 15:30], ret_tm, 27, at(1, 0))
    back_br = copy(dbuf.at[1, 0:15, 0:16], ret_br, 28, at(-1, 0))
    back_bl = copy(dbuf.at[1, 0:15, 16:32], ret_bl, 29, at(-1, 1))
    back_tl = copy(dbuf.at[1, 15:30, 16:32], ret_tl, 30, at(0, 1))

    pad1 = jnp.zeros((1, D), BF)
    pad2 = jnp.zeros((2, D), BF)
    for n, ref in ((0, x_ref), (1, g_ref)):
        for i in range(15):
            s_a[n, i, 0:30, :] = ref[0, i, 15:45, :]
            s_a[n, i, 30:32, :] = pad2
            s_tl[n, i, 0:15, :] = ref[0, i, 0:15, :]
            s_tl[n, i, 15:16, :] = pad1
            s_br[n, i, 0:15, :] = ref[0, 15 + i, 45:60, :]
            s_br[n, i, 15:16, :] = pad1
            s_bl[n, i, 0:15, :] = ref[0, 15 + i, 0:15, :]
            s_bl[n, i, 15:16, :] = pad1
    pl.semaphore_wait(barrier, len(peers))

    @pl.when(core == 0)
    def _():
        halo_a.start()
        halo_tl.start()
        halo_bl.start()

    @pl.when(core == 1)
    def _():
        halo_br.start()

    for n, ref in ((0, x_ref), (1, g_ref)):
        for i in range(15):
            buf[0, n, i, 0:30, :] = ref[0, 15 + i, 15:45, :]
            buf[0, n, i, 30:32, :] = pad2
            buf[1, n, 15 + i, 0:15, :] = ref[0, i, 45:60, :]
            buf[1, n, 15 + i, 15:16, :] = pad1

    gain = gain_ref[...].reshape(1, D)
    for n in range(9):
        w_t[n * 128:(n + 1) * 128, :] = w_ref[:, n * 128:(n + 1) * 128].T
    gp[...] = jnp.zeros_like(gp)
    for n in range(3):
        total[n, 0:1152, :] = jnp.zeros((1152, 128), F32)
    nl[KC:, :] = jnp.zeros((QC - KC, D), BF)
    gs[KC:, :] = jnp.zeros((QC - KC, D), BF)
    dqkv_t[:, :, KC:] = jnp.zeros((18, 64, QC - KC), BF)
    half = jnp.zeros((64, QC), BF)
    one = (lax.broadcasted_iota(jnp.int32, (128, QC), 0) == 0).astype(F32).astype(BF)
    rest = jnp.zeros((128, QC), BF)
    for h in range(HEADS):
        o = (h % 2) * 64
        q_aug[h, 64 - o:128 - o, :] = half
        b_aug[h, 64 - o:128 - o, :] = half
        q_aug[h, 128:256, :] = one
        b_aug[h, 128:256, :] = rest
    row = lax.broadcasted_iota(jnp.int32, (KC, 128), 0)
    lane = lax.broadcasted_iota(jnp.int32, (KC, 128), 1)
    ones = jnp.where(lane < 2, 1.0, 0.0).astype(BF)
    for j in range(3):
        v_aug[j, :, 128:256] = ones

    def head(h, carry):
        j = h // 2
        o = pl.multiple_of(lax.rem(h, 2) * 64, 64)
        acc = jnp.zeros((8, QC), F32)
        for k in range(0, KC, CK):
            e = jnp.exp(dot(k_aug[j, k:k + CK, :], q_aug[h]))
            p32[k:k + CK, :] = e
            acc = acc + jnp.sum(e.reshape(CK // 8, 8, QC), axis=0)
        r = 1.0 / jnp.sum(acc, axis=0, keepdims=True)
        for k in range(0, KC, CK):
            p = p32[k:k + CK, :] * r
            p32[k:k + CK, :] = p
            p_low[k:k + CK, :] = p.astype(BF)
        a = dot(qkv_t[12 + h][:, 0:KC], p_low[...])
        att_t[h] = a.astype(BF)
        less = -jnp.sum(a * b_aug[h, pl.ds(o, 64), :].astype(F32), axis=0, keepdims=True)
        high = less.astype(BF).astype(F32)
        r16 = lax.broadcasted_iota(jnp.int32, (16, QC), 0)
        b_aug[h, 128:144, :] = jnp.where(r16 == 0, high, jnp.where(r16 == 1, less - high, 0.0)).astype(BF)
        for k in range(0, KC, CK):
            dprobs = dot(v_aug[j, k:k + CK, :], b_aug[h])
            ds_low[k:k + CK, :] = (p32[k:k + CK, :] * dprobs).astype(BF)
        dqkv_t[h] = (dot(qkv_t[6 + h][:, 0:KC], ds_low[...]) * 0.125).astype(BF)
        dqkv_t[6 + h, :, 0:KC] = dot(qkv_t[h], ds_low[...], NT).astype(BF)
        dqkv_t[12 + h, :, 0:KC] = dot(b_aug[h, pl.ds(o, 64), :], p_low[...], NT).astype(BF)
        return carry

    def arrive(kind):
        @pl.when(kind == 0)
        def _():
            halo_a.wait_recv()

        @pl.when(kind == 1)
        def _():
            halo_br.wait_recv()
            halo_tl.wait_recv()
            halo_bl.wait_recv()

    def finish(kind):
        for t in range(4):
            n = 256 if t < 3 else 192
            rows = slice(t * 256, t * 256 + 256)
            dn = dot(w_ref[...], dqkv_t[:, :, rows].reshape(3 * D, 256)).T[0:n] * gain
            own = slice(t * 256, t * 256 + n)
            norm = normed[own, :]
            m1 = jnp.sum(dn, axis=1, keepdims=True) * (1 / D)
            m2 = jnp.sum(dn * norm, axis=1, keepdims=True) * (1 / D)
            d = (rstd_s[own, 0:1] * (dn - m1 - norm * m2)).astype(BF)
            dbuf[kind, t * 8:t * 8 + n // 32] = d.reshape(n // 32, 32, D)

        @pl.when(kind == 0)
        def _():
            back_tm.start()

        @pl.when(kind == 1)
        def _():
            back_br.start()
            back_bl.start()
            back_tl.start()

    def window(i, carry):
        kind = lax.rem(core + i, 2)
        edge = jnp.where(kind == 0, lat == 15, lat == 0)
        arrive(kind)

        @pl.when((i == 0) & (core == 0))
        def _():
            halo_br.start()

        @pl.when((i == 0) & (core == 1))
        def _():
            halo_a.start()
            halo_tl.start()
            halo_bl.start()

        @pl.when(edge)
        def _():
            buf[kind, :, 15:30, :, :] = jnp.zeros((2, 15, 32, D), BF)

        def norm(n, c):
            rows = pl.ds(pl.multiple_of(n * 96, 96), 96)
            cells = pl.ds(n * 3, 3)
            x = buf[kind, 0, cells].reshape(96, D).astype(F32)
            gs[rows, :] = buf[kind, 1, cells].reshape(96, D)
            centred = x - jnp.sum(x, axis=1, keepdims=True) * (1 / D)
            rstd = lax.rsqrt(jnp.sum(centred * centred, axis=1, keepdims=True) * (1 / D) + EPS)
            v = centred * rstd
            normed[rows, :] = v
            rstd_s[rows, :] = jnp.broadcast_to(rstd, (96, 128))
            nl[rows, :] = (v * gain).astype(BF)
            return c

        lax.fori_loop(0, KC // 96, norm, 0)
        q = (dot(w_t[0:D, :], nl[...], NT).astype(BF).astype(F32) * 0.125).astype(BF)
        qkv_t[0:6] = q.reshape(6, 64, QC)
        for part in (1, 2):
            rows = slice(part * D, (part + 1) * D)
            qkv_t[part * 6:part * 6 + 6] = dot(w_t[rows, :], nl[...], NT).astype(BF).reshape(6, 64, QC)
        bt = dot(wp_ref[...], gs[...], NT).astype(BF).reshape(6, 64, QC)
        for h in range(HEADS):
            o = (h % 2) * 64
            q_aug[h, o:o + 64, :] = qkv_t[h]
            b_aug[h, o:o + 64, :] = bt[h]
        slot = jnp.where(kind == 0, row & 31, (row & 15) + 15)
        bad = (slot >= 30) | ((row >= KC // 2) & edge)
        bias = jnp.where((lane == 0) & bad, -30000.0, 0.0).astype(BF)
        for j in range(3):
            cols = slice(D + j * 128, D + (j + 1) * 128)
            k_aug[j, :, 0:128] = dot(nl[0:KC, :], w_ref[:, cols]).astype(BF)
            cols = slice(2 * D + j * 128, 2 * D + (j + 1) * 128)
            v_aug[j, :, 0:128] = dot(nl[0:KC, :], w_ref[:, cols]).astype(BF)
            k_aug[j, :, 128:256] = bias
        lax.fori_loop(0, HEADS, head, 0)
        dw = dot(dqkv_t[...].reshape(3 * D, QC), nl[...])
        for n in range(3):
            total[n, 0:1152, :] += dw[:, n * 128:(n + 1) * 128]
        gp[...] += dot(att_t[...].reshape(D, QC), gs[...])

        @pl.when(i == 0)
        def _():
            finish(kind)

        return carry

    lax.fori_loop(0, 2, window, 0)

    for n in range(3):
        total[n, 1152:1536, :] = gp[n * 128:(n + 1) * 128, :].T

    def gather(at_lon, j):
        first, step = (9 * at_lon + j, 72) if j < 9 else (1152 + 3 * at_lon + j - 9, 24)
        return jnp.concatenate([total[n, pl.ds(first, 16, stride=step), :] for n in range(3)], axis=1)

    core_copies = [copy(core_send.at[i], core_recv.at[i], i, partner) for i in range(4)]
    for i in range(4):
        for j in range(12):
            core_send[i, j * 16:(j + 1) * 16, :] = gather(2 * i + 1 - core, j).astype(BF)
        core_copies[i].start()
    for i in range(4):
        for j in range(12):
            core_own[i, j * 16:(j + 1) * 16, :] = gather(2 * i + core, j)
    finish(1 - core)
    for i in range(4):
        core_copies[i].wait()
        core_own[i] = core_own[i] + core_recv[i].astype(F32)
    y_copies = []
    for k in range(1, 4):
        t = lax.rem(y + k, 4)
        y_send[k - 1] = core_own[t].astype(BF)
        c = copy(y_send.at[k - 1], y_recv.at[k - 1], 3 + k, {"y": t})
        c.start()
        y_copies.append(c)
    back_tm.wait_recv()
    back_br.wait_recv()
    back_bl.wait_recv()
    back_tl.wait_recv()
    for i in range(15):
        for r, c0, c1, part in (
                (i, 0, 15, ret_tl[i, 0:15, :]), (i, 15, 45, ret_tm[i, 0:30, :]),
                (i, 45, 60, dbuf[1, 15 + i, 0:15, :]), (15 + i, 0, 15, ret_bl[i, 0:15, :]),
                (15 + i, 15, 45, dbuf[0, i, 0:30, :]), (15 + i, 45, 60, ret_br[i, 0:15, :])):
            out_ref[0, r, c0:c1, :] = (g_ref[0, r, c0:c1, :].astype(F32) + part.astype(F32)).astype(BF)
    for k in range(3):
        y_copies[k].wait()
    mine = core_own[y] + y_recv[0].astype(F32) + y_recv[1].astype(F32) + y_recv[2].astype(F32)
    for n in range(3):
        y_own[n] = mine[:, n * 128:(n + 1) * 128]

    def strided(first):
        return jnp.concatenate([y_own[n, pl.ds(first, 12, stride=16), :] for n in range(3)], axis=1)

    spare = jnp.zeros((4, D), F32)
    for t in range(16):
        lat_send[t] = jnp.concatenate([strided(t), spare], axis=0).astype(BF)
    lat_copies = []
    for k in range(1, 16):
        c = copy(lat_send.at[lax.rem(lat + k, 16)], lat_recv.at[k - 1], 6 + k, at(k, 0))
        c.start()
        lat_copies.append(c)
    own = strided(lat)
    for k in range(15):
        lat_copies[k].wait()
        own = own + lat_recv[k, 0:12, :].astype(F32)
    dp_send[...] = jnp.concatenate([own, spare], axis=0)
    c = copy(dp_send, dp_recv, 22, {"dp": 1 - dp})
    c.start()
    c.wait()
    sums_ref[...] = dp_send[...] + dp_recv[...]
    for c in (halo_a, halo_br, halo_tl, halo_bl, back_tm, back_br, back_bl, back_tl):
        c.wait_send()


def per_device(hidden_in, grad_out, norm_gain, w_qkv, w_proj):
    V = pl.BlockSpec(memory_space=pltpu.VMEM)
    scratch = [
        ((2, 2, 30, 32, D), BF), ((2, 15, 32, D), BF), ((2, 15, 16, D), BF), ((2, 15, 16, D), BF),
        ((2, 15, 16, D), BF), ((2, 30, 32, D), BF), ((15, 32, D), BF), ((15, 16, D), BF), ((15, 16, D), BF),
        ((15, 16, D), BF),
        ((3 * D, D), BF), ((KC, D), F32), ((KC, 128), F32), ((QC, D), BF), ((QC, D), BF), ((6, 256, QC), BF),
        ((6, 256, QC), BF), ((3, KC, 256), BF), ((3, KC, 256), BF), ((18, 64, QC), BF), ((KC, QC), F32),
        ((KC, QC), BF), ((KC, QC), BF), ((18, 64, QC), BF), ((6, 64, QC), BF),
        ((D, D), F32), ((3, 1536, 128), F32), ((4, 192, D), BF), ((4, 192, D), BF), ((4, 192, D), F32),
        ((3, 192, D), BF), ((3, 192, D), BF), ((3, 192, 128), F32), ((16, 16, D), BF), ((15, 16, D), BF),
        ((16, D), F32), ((16, D), F32),
    ]
    grad_in, sums = pl.pallas_call(
        kernel,
        out_shape=(jax.ShapeDtypeStruct(grad_out.shape, BF), jax.ShapeDtypeStruct((16, D), F32)),
        in_specs=[V] * 5,
        out_specs=(V, V),
        scratch_shapes=[pltpu.VMEM(s, d) for s, d in scratch] + [pltpu.SemaphoreType.DMA((31,))] * 2,
        compiler_params=pltpu.CompilerParams(
            vmem_limit_bytes=63 * 1024 * 1024, collective_id=0, has_side_effects=True),
        name="block_backward",
    )(hidden_in, grad_out, norm_gain, w_qkv, w_proj)
    mine = lax.dynamic_slice_in_dim(sums, lax.axis_index("dp") * 192, 192, axis=1)[:12].T
    factor = 460800.0 ** -0.5
    return grad_in, mine[:, :9] * factor, mine[:, 9:] * factor


def solution(mesh):
    split = Mesh(mesh.devices.reshape(2, 2, 8, 4, 2), ("dp", "xl", "z", "y", "core"))
    return jax.shard_map(
        per_device,
        mesh=split,
        in_specs=(P("dp", LAT, LON, None), P("dp", LAT, LON, None), P(), P(), P()),
        out_specs=(P("dp", LAT, LON, None), P("dp", BOTH), P("dp", BOTH)),
        check_vma=False,
    )
```

time: 941 us -> 106 us (0.11)
  waiting for transfers between devices: 681 us -> 0 us
  matrix products: 158 us -> 0 us
  Pallas kernels: 0 us -> 100 us
  local copies, waits for them, and re-layouts: 54.5 us -> 3.45 us
  other arithmetic: 20.4 us -> 1.21 us
  between operations: 14.7 us -> 0.65 us
  starting transfers between devices: 10.1 us -> 0 us
    unnamed x7 -> x0, waiting for transfers between devices: 610 us -> none
    dot_general x82 -> x0, matrix products: 158 us -> none  [the longest x12 31 us: attend_head(): jnp.dot(attention_low.T, grad_rows, preferred_element_type=jnp.float32)]
    pallas_call x0 -> x1, Pallas kernels: none -> 100 us  [per_device(): pl.pallas_call(kernel, out_shape=(jax.ShapeDtypeStruct(grad_out.shape, BF...]
    ppermute x4 -> x0, waiting for transfers between devices: 54.7 us -> none  [the longest x2 46.7 us: passed_along(): return lax.ppermute(x, axis, pairs)]
    reduce_scatter x1 -> x0, waiting for transfers between devices: 16.4 us -> none  [scatter_pairs(): pieces = lax.psum_scatter(pieces, core, scatter_dimension=0, tiled=True)]
    slice x13 -> x0, local copies, waits for them, and re-layouts: 15.4 us -> none  [the longest x4 7.11 us: window_grads(): qkv[:, 2 * model_width:]]
    convert_element_type x14 -> x0, other arithmetic: 15.1 us -> none  [the longest x12 13.1 us: attend_head(): dscores = (attention * (dprobs - row_total) * scaling).astype(jnp.bfloat16)]
    ppermute x4 -> x0, starting transfers between devices: 9.93 us -> none  [the longest x2 5.37 us: shifted_2(): return lax.ppermute(value, axis, pairs)]
  transfers between devices with their start and end apart: 8 -> 0, of which waited for: 7 -> 0; matrix products, arithmetic and copies ran while one was open for 2% -> 0% of each run, Pallas kernels for 0% -> 0%
where the time goes in v2:
time: 106 us
  Pallas kernels  100 us (94%)
  local copies, waits for them, and re-layouts  3.45 us (3%)
  other arithmetic  1.21 us (1%)
    pallas_call x1, Pallas kernels, per_device(): pl.pallas_call(kernel, out_shape=(jax.ShapeDtypeStruct(grad_out.shape, BF...  100 us
    unnamed x1, local copies, waits for them, and re-layouts  2.63 us

profile of v2, /device:TPU:1, one launch (start us, length us, event | category | flops | bytes accessed | tf_op | source)
XLA Modules:
  0.0 105.6 jit_solution(16884056246350279803)
XLA Ops:
  0.6 100.3 %block_backward.1 = (bf16[1,30,60,384]{3,2,1,0:T(8,128)(2,1)}, f32[16,384]{1,0:T(8,128)}) custom-call(bf16[1,30,60,384]{3,2,1,0:T(8,128)(2,1)} %x_ref.1, bf16[1,30,60,384]{3,2,1,0:T(8,128)(2,1)} %g_ref.1, f32[384]{0:T(512)} %gain_ref.1, bf16[384,1152]{1,0:T(8,128)(2,1)} %w_ref.1, bf16[384,384]{1,0:T(8,128)(2,1)} %wp_ref.1), custom_call_target="tpu_custom_call" | custom-call | tf_op jit(solution)/shard_map/block_backward/pallas_call | solution.py:325
  101.0 0.8 dynamic-slice_bitcast_fusion
  101.8 0.6 slice_multiply_fusion
  102.4 0.6 slice_multiply_fusion.1
  103.0 2.6 %copy.9 = bf16[1,30,60,384]{3,2,1,0:T(8,128)(2,1)} copy(bf16[1,30,60,384]{3,2,1,0:T(8,128)(2,1)} %get-tuple-element.10) | data formatting | bytes 2764800

commit v3 on v2

--- a/solution.py
+++ b/solution.py
@@ -26,12 +26,17 @@
     return lax.dot_general(a, b, dims, preferred_element_type=F32)
 
 
-def kernel(x_ref, g_ref, gain_ref, w_ref, wp_ref, out_ref, sums_ref,
+def kernel(x_hbm, g_hbm, gain_ref, w_ref, wp_ref, out_ref, qkv_ref, proj_ref,
+           x_ref, g_ref,
            buf, s_a, s_br, s_tl, s_bl, dbuf, ret_tm, ret_br, ret_bl, ret_tl,
            w_t, normed, rstd_s, nl, gs, q_aug, b_aug, k_aug, v_aug, qkv_t, p32, p_low, ds_low, dqkv_t, att_t,
            gp, total, core_send, core_recv, core_own, y_send, y_recv, y_own, lat_send, lat_recv,
-           dp_send, dp_recv, send_sems, recv_sems):
+           dp_send, dp_recv, send_sems, recv_sems, load_sems):
     dp, xl, z, y, core = (lax.axis_index(n) for n in ("dp", "xl", "z", "y", "core"))
+    loads = [pltpu.make_async_copy(src, dst, load_sems.at[n]) for n, (src, dst) in enumerate((
+        (x_hbm.at[0], x_ref), (g_hbm.at[0], g_ref)))]
+    for load in loads:
+        load.start()
     lat = xl * 8 + z
     lon = y * 2 + core
 
@@ -53,44 +58,46 @@
     for peer in peers:
         pl.semaphore_signal(barrier, inc=1, device_id=peer, device_id_type=MESH)
 
-    halo_a = copy(s_a, buf.at[0, :, 15:30], 23, at(-1, 0))
-    halo_br = copy(s_br, buf.at[1, :, 0:15, 0:16], 24, at(1, 0))
-    halo_tl = copy(s_tl, buf.at[1, :, 15:30, 16:32], 25, at(0, -1))
-    halo_bl = copy(s_bl, buf.at[1, :, 0:15, 16:32], 26, at(1, -1))
-    back_tm = copy(dbuf.at[0, 15:30], ret_tm, 27, at(1, 0))
-    back_br = copy(dbuf.at[1, 0:15, 0:16], ret_br, 28, at(-1, 0))
-    back_bl = copy(dbuf.at[1, 0:15, 16:32], ret_bl, 29, at(-1, 1))
-    back_tl = copy(dbuf.at[1, 15:30, 16:32], ret_tl, 30, at(0, 1))
+    halo_a = [copy(s_a.at[n], buf.at[0, n, 15:30], 26 + n, at(-1, 0)) for n in range(2)]
+    halo_br = [copy(s_br.at[n], buf.at[1, n, 0:15, 0:16], 28 + n, at(1, 0)) for n in range(2)]
+    halo_tl = [copy(s_tl.at[n], buf.at[1, n, 15:30, 16:32], 30 + n, at(0, -1)) for n in range(2)]
+    halo_bl = [copy(s_bl.at[n], buf.at[1, n, 0:15, 16:32], 32 + n, at(1, -1)) for n in range(2)]
+    back_tm = copy(dbuf.at[0, 15:30], ret_tm, 34, at(1, 0))
+    back_br = copy(dbuf.at[1, 0:15, 0:16], ret_br, 35, at(-1, 0))
+    back_bl = copy(dbuf.at[1, 0:15, 16:32], ret_bl, 36, at(-1, 1))
+    back_tl = copy(dbuf.at[1, 15:30, 16:32], ret_tl, 37, at(0, 1))
 
     pad1 = jnp.zeros((1, D), BF)
     pad2 = jnp.zeros((2, D), BF)
     for n, ref in ((0, x_ref), (1, g_ref)):
+        loads[n].wait()
         for i in range(15):
-            s_a[n, i, 0:30, :] = ref[0, i, 15:45, :]
+            s_a[n, i, 0:30, :] = ref[i, 15:45, :]
             s_a[n, i, 30:32, :] = pad2
-            s_tl[n, i, 0:15, :] = ref[0, i, 0:15, :]
+            s_tl[n, i, 0:15, :] = ref[i, 0:15, :]
             s_tl[n, i, 15:16, :] = pad1
-            s_br[n, i, 0:15, :] = ref[0, 15 + i, 45:60, :]
+            s_br[n, i, 0:15, :] = ref[15 + i, 45:60, :]
             s_br[n, i, 15:16, :] = pad1
-            s_bl[n, i, 0:15, :] = ref[0, 15 + i, 0:15, :]
+            s_bl[n, i, 0:15, :] = ref[15 + i, 0:15, :]
             s_bl[n, i, 15:16, :] = pad1
-    pl.semaphore_wait(barrier, len(peers))
-
-    @pl.when(core == 0)
-    def _():
-        halo_a.start()
-        halo_tl.start()
-        halo_bl.start()
-
-    @pl.when(core == 1)
-    def _():
-        halo_br.start()
+        if n == 0:
+            pl.semaphore_wait(barrier, len(peers))
+
+        @pl.when(core == 0)
+        def _():
+            halo_a[n].start()
+            halo_tl[n].start()
+            halo_bl[n].start()
+
+        @pl.when(core == 1)
+        def _():
+            halo_br[n].start()
 
     for n, ref in ((0, x_ref), (1, g_ref)):
         for i in range(15):
-            buf[0, n, i, 0:30, :] = ref[0, 15 + i, 15:45, :]
+            buf[0, n, i, 0:30, :] = ref[15 + i, 15:45, :]
             buf[0, n, i, 30:32, :] = pad2
-            buf[1, n, 15 + i, 0:15, :] = ref[0, i, 45:60, :]
+            buf[1, n, 15 + i, 0:15, :] = ref[i, 45:60, :]
             buf[1, n, 15 + i, 15:16, :] = pad1
 
     gain = gain_ref[...].reshape(1, D)
@@ -144,16 +151,21 @@
         dqkv_t[12 + h, :, 0:KC] = dot(b_aug[h, pl.ds(o, 64), :], p_low[...], NT).astype(BF)
         return carry
 
-    def arrive(kind):
+    def arrive(kind, n):
         @pl.when(kind == 0)
         def _():
-            halo_a.wait_recv()
+            halo_a[n].wait_recv()
 
         @pl.when(kind == 1)
         def _():
-            halo_br.wait_recv()
-            halo_tl.wait_recv()
-            halo_bl.wait_recv()
+            halo_br[n].wait_recv()
+            halo_tl[n].wait_recv()
+            halo_bl[n].wait_recv()
+
+    def clear(kind, n, edge):
+        @pl.when(edge)
+        def _():
+            buf[kind, n, 15:30, :, :] = jnp.zeros((15, 32, D), BF)
 
     def finish(kind):
         for t in range(4):
@@ -180,27 +192,13 @@
     def window(i, carry):
         kind = lax.rem(core + i, 2)
         edge = jnp.where(kind == 0, lat == 15, lat == 0)
-        arrive(kind)
-
-        @pl.when((i == 0) & (core == 0))
-        def _():
-            halo_br.start()
-
-        @pl.when((i == 0) & (core == 1))
-        def _():
-            halo_a.start()
-            halo_tl.start()
-            halo_bl.start()
-
-        @pl.when(edge)
-        def _():
-            buf[kind, :, 15:30, :, :] = jnp.zeros((2, 15, 32, D), BF)
+        arrive(kind, 0)
+        clear(kind, 0, edge)
 
         def norm(n, c):
             rows = pl.ds(pl.multiple_of(n * 96, 96), 96)
             cells = pl.ds(n * 3, 3)
             x = buf[kind, 0, cells].reshape(96, D).astype(F32)
-            gs[rows, :] = buf[kind, 1, cells].reshape(96, D)
             centred = x - jnp.sum(x, axis=1, keepdims=True) * (1 / D)
             rstd = lax.rsqrt(jnp.sum(centred * centred, axis=1, keepdims=True) * (1 / D) + EPS)
             v = centred * rstd
@@ -215,6 +213,22 @@
         for part in (1, 2):
             rows = slice(part * D, (part + 1) * D)
             qkv_t[part * 6:part * 6 + 6] = dot(w_t[rows, :], nl[...], NT).astype(BF).reshape(6, 64, QC)
+        arrive(kind, 1)
+        clear(kind, 1, edge)
+
+        @pl.when((i == 0) & (core == 0))
+        def _():
+            for n in range(2):
+                halo_br[n].start()
+
+        @pl.when((i == 0) & (core == 1))
+        def _():
+            for n in range(2):
+                halo_a[n].start()
+                halo_tl[n].start()
+                halo_bl[n].start()
+
+        gs[0:KC, :] = buf[kind, 1].reshape(KC, D)
         bt = dot(wp_ref[...], gs[...], NT).astype(BF).reshape(6, 64, QC)
         for h in range(HEADS):
             o = (h % 2) * 64
@@ -250,25 +264,38 @@
         first, step = (9 * at_lon + j, 72) if j < 9 else (1152 + 3 * at_lon + j - 9, 24)
         return jnp.concatenate([total[n, pl.ds(first, 16, stride=step), :] for n in range(3)], axis=1)
 
+    turns = [lax.rem(y + k, 4) for k in (2, 1, 3, 0)]
     core_copies = [copy(core_send.at[i], core_recv.at[i], i, partner) for i in range(4)]
     for i in range(4):
         for j in range(12):
-            core_send[i, j * 16:(j + 1) * 16, :] = gather(2 * i + 1 - core, j).astype(BF)
+            core_send[i, j * 16:(j + 1) * 16, :] = gather(2 * turns[i] + 1 - core, j).astype(BF)
         core_copies[i].start()
     for i in range(4):
         for j in range(12):
-            core_own[i, j * 16:(j + 1) * 16, :] = gather(2 * i + core, j)
+            core_own[i, j * 16:(j + 1) * 16, :] = gather(2 * turns[i] + core, j)
     finish(1 - core)
+    up, down = {"y": turns[1]}, {"y": turns[2]}
+    y_copies = [copy(y_send.at[n], y_recv.at[n], 4 + n, (up, down)[n % 2]) for n in range(6)]
+    first, second = slice(0, 96), slice(96, 192)
+
+    def send_y(n, value):
+        y_send[n] = value.astype(BF)
+        y_copies[n].start()
+
     for i in range(4):
         core_copies[i].wait()
         core_own[i] = core_own[i] + core_recv[i].astype(F32)
-    y_copies = []
-    for k in range(1, 4):
-        t = lax.rem(y + k, 4)
-        y_send[k - 1] = core_own[t].astype(BF)
-        c = copy(y_send.at[k - 1], y_recv.at[k - 1], 3 + k, {"y": t})
-        c.start()
-        y_copies.append(c)
+        if i == 0:
+            send_y(0, core_own[0, first])
+            send_y(1, core_own[0, second])
+        if i == 1:
+            send_y(2, core_own[1, second])
+        if i == 2:
+            send_y(3, core_own[2, first])
+    y_copies[0].wait()
+    send_y(4, core_own[1, first] + y_recv[0].astype(F32))
+    y_copies[1].wait()
+    send_y(5, core_own[2, second] + y_recv[1].astype(F32))
     back_tm.wait_recv()
     back_br.wait_recv()
     back_bl.wait_recv()
@@ -278,12 +305,14 @@
                 (i, 0, 15, ret_tl[i, 0:15, :]), (i, 15, 45, ret_tm[i, 0:30, :]),
                 (i, 45, 60, dbuf[1, 15 + i, 0:15, :]), (15 + i, 0, 15, ret_bl[i, 0:15, :]),
                 (15 + i, 15, 45, dbuf[0, i, 0:30, :]), (15 + i, 45, 60, ret_br[i, 0:15, :])):
-            out_ref[0, r, c0:c1, :] = (g_ref[0, r, c0:c1, :].astype(F32) + part.astype(F32)).astype(BF)
-    for k in range(3):
-        y_copies[k].wait()
-    mine = core_own[y] + y_recv[0].astype(F32) + y_recv[1].astype(F32) + y_recv[2].astype(F32)
+            out_ref[0, r, c0:c1, :] = (g_ref[r, c0:c1, :].astype(F32) + part.astype(F32)).astype(BF)
+    for n in range(2, 6):
+        y_copies[n].wait()
+    low = core_own[3, first] + y_recv[4].astype(F32) + y_recv[3].astype(F32)
+    high = core_own[3, second] + y_recv[2].astype(F32) + y_recv[5].astype(F32)
     for n in range(3):
-        y_own[n] = mine[:, n * 128:(n + 1) * 128]
+        y_own[n, first] = low[:, n * 128:(n + 1) * 128]
+        y_own[n, second] = high[:, n * 128:(n + 1) * 128]
 
     def strided(first):
         return jnp.concatenate([y_own[n, pl.ds(first, 12, stride=16), :] for n in range(3)], axis=1)
@@ -293,7 +322,7 @@
         lat_send[t] = jnp.concatenate([strided(t), spare], axis=0).astype(BF)
     lat_copies = []
     for k in range(1, 16):
-        c = copy(lat_send.at[lax.rem(lat + k, 16)], lat_recv.at[k - 1], 6 + k, at(k, 0))
+        c = copy(lat_send.at[lax.rem(lat + k, 16)], lat_recv.at[k - 1], 9 + k, at(k, 0))
         c.start()
         lat_copies.append(c)
     own = strided(lat)
@@ -301,17 +330,22 @@
         lat_copies[k].wait()
         own = own + lat_recv[k, 0:12, :].astype(F32)
     dp_send[...] = jnp.concatenate([own, spare], axis=0)
-    c = copy(dp_send, dp_recv, 22, {"dp": 1 - dp})
+    c = copy(dp_send, dp_recv, 25, {"dp": 1 - dp})
     c.start()
     c.wait()
-    sums_ref[...] = dp_send[...] + dp_recv[...]
-    for c in (halo_a, halo_br, halo_tl, halo_bl, back_tm, back_br, back_bl, back_tl):
+    factor = 460800.0 ** -0.5
+    both = (dp_send[...] + dp_recv[...]) * factor
+    mine = jnp.where(dp == 0, both, pltpu.roll(both, 192, 1))
+    qkv_ref[...] = mine[0:9, 0:192]
+    proj_ref[...] = mine[9:12, 0:192]
+    for c in (*halo_a, *halo_br, *halo_tl, *halo_bl, back_tm, back_br, back_bl, back_tl):
         c.wait_send()
 
 
 def per_device(hidden_in, grad_out, norm_gain, w_qkv, w_proj):
     V = pl.BlockSpec(memory_space=pltpu.VMEM)
     scratch = [
+        ((30, 60, D), BF), ((30, 60, D), BF),
         ((2, 2, 30, 32, D), BF), ((2, 15, 32, D), BF), ((2, 15, 16, D), BF), ((2, 15, 16, D), BF),
         ((2, 15, 16, D), BF), ((2, 30, 32, D), BF), ((15, 32, D), BF), ((15, 16, D), BF), ((15, 16, D), BF),
         ((15, 16, D), BF),
@@ -319,22 +353,23 @@
         ((6, 256, QC), BF), ((3, KC, 256), BF), ((3, KC, 256), BF), ((18, 64, QC), BF), ((KC, QC), F32),
         ((KC, QC), BF), ((KC, QC), BF), ((18, 64, QC), BF), ((6, 64, QC), BF),
         ((D, D), F32), ((3, 1536, 128), F32), ((4, 192, D), BF), ((4, 192, D), BF), ((4, 192, D), F32),
-        ((3, 192, D), BF), ((3, 192, D), BF), ((3, 192, 128), F32), ((16, 16, D), BF), ((15, 16, D), BF),
+        ((6, 96, D), BF), ((6, 96, D), BF), ((3, 192, 128), F32), ((16, 16, D), BF), ((15, 16, D), BF),
         ((16, D), F32), ((16, D), F32),
     ]
-    grad_in, sums = pl.pallas_call(
+    H = pl.BlockSpec(memory_space=pltpu.HBM)
+    grad_in, qkv, proj = pl.pallas_call(
         kernel,
-        out_shape=(jax.ShapeDtypeStruct(grad_out.shape, BF), jax.ShapeDtypeStruct((16, D), F32)),
-        in_specs=[V] * 5,
-        out_specs=(V, V),
-        scratch_shapes=[pltpu.VMEM(s, d) for s, d in scratch] + [pltpu.SemaphoreType.DMA((31,))] * 2,
+        out_shape=(jax.ShapeDtypeStruct(grad_out.shape, BF), jax.ShapeDtypeStruct((9, 192), F32),
+                   jax.ShapeDtypeStruct((3, 192), F32)),
+        in_specs=[H, H, V, V, V],
+        out_specs=(V, V, V),
+        scratch_shapes=[pltpu.VMEM(s, d) for s, d in scratch] + [pltpu.SemaphoreType.DMA((38,))] * 2
+        + [pltpu.SemaphoreType.DMA((2,))],
         compiler_params=pltpu.CompilerParams(
-            vmem_limit_bytes=63 * 1024 * 1024, collective_id=0, has_side_effects=True),
+            vmem_limit_bytes=50 * 1024 * 1024, collective_id=0, has_side_effects=True),
         name="block_backward",
     )(hidden_in, grad_out, norm_gain, w_qkv, w_proj)
-    mine = lax.dynamic_slice_in_dim(sums, lax.axis_index("dp") * 192, 192, axis=1)[:12].T
-    factor = 460800.0 ** -0.5
-    return grad_in, mine[:, :9] * factor, mine[:, 9:] * factor
+    return grad_in, qkv.T, proj.T
 
 
 def solution(mesh):

time: 106 us -> 101 us (0.953)
  Pallas kernels: 100 us -> 94.6 us
  local copies, waits for them, and re-layouts: 3.45 us -> 5.11 us
  other arithmetic: 1.21 us -> 0 us
    pallas_call x1, Pallas kernels: 100 us -> 94.6 us  [per_device(): pl.pallas_call(kernel, out_shape=(jax.ShapeDtypeStruct(grad_out.shape, BF...]
    unnamed x1 -> x9, local copies, waits for them, and re-layouts: 2.63 us -> 5.11 us
    mul x2 -> x0, other arithmetic: 1.21 us -> none  [per_device(): return (grad_in, mine[:, :9] * factor, mine[:, 9:] * factor)]
where the time goes in v3:
time: 101 us; the launch traced here: 100 us
  Pallas kernels  94.6 us (94%)
  local copies, waits for them, and re-layouts  5.11 us (5%)
    pallas_call x1, Pallas kernels, per_device(): pl.pallas_call(kernel, out_shape=(jax.ShapeDtypeStruct(grad_out.shape, BF...  94.6 us
    unnamed x9, local copies, waits for them, and re-layouts  5.11 us

profile of v3, /device:TPU:1, one launch (start us, length us, event | category | flops | bytes accessed | tf_op | source)
XLA Modules:
  0.0 100.3 jit_solution(9285010932508178605)
XLA Ops:
  0.6 0.0 copy-start
  0.6 1.2 %copy-done = bf16[384,1152]{1,0:T(8,128)(2,1)S(1)} copy-done((bf16[384,1152]{1,0:T(8,128)(2,1)S(1)}, bf16[384,1152]{1,0:T(8,128)(2,1)}, u32[]{:S(2)}) %copy-start) | copy-done | bytes 884760
  1.8 0.0 copy-start.1
  1.8 1.0 copy-done.1
  2.8 0.0 copy-start.2
  2.8 0.7 copy-done.2
  3.4 94.6 %block_backward.1 = (bf16[1,30,60,384]{3,2,1,0:T(8,128)(2,1)S(1)}, f32[9,192]{1,0:T(8,128)S(1)}, f32[3,192]{1,0:T(4,128)S(1)}) custom-call(bf16[1,30,60,384]{3,2,1,0:T(8,128)(2,1)} %x_hbm.1, bf16[1,30,60,384]{3,2,1,0:T(8,128)(2,1)} %g_hbm.1, f32[384]{0:T(512)S(1)} %copy-done.2, bf16[384,1152]{1,0:T(8,128)(2,1)S(1)} %copy-done, bf16[384,384]{1,0:T(8,128)(2,1)S(1)} %copy-done.1), custom_call_target="tpu_custom_call" | custom-call | tf_op jit(solution)/shard_map/block_backward/pallas_call | solution.py:360
  98.0 1.1 %copy.11 = bf16[1,30,60,384]{3,2,1,0:T(8,128)(2,1)} copy(bf16[1,30,60,384]{3,2,1,0:T(8,128)(2,1)S(1)} %get-tuple-element.12) | data formatting | bytes 2764800
  99.1 0.6 copy.12
  99.7 0.6 copy.13
Async XLA Ops:
  0.6 1.2 %copy-start = (bf16[384,1152]{1,0:T(8,128)(2,1)S(1)}, bf16[384,1152]{1,0:T(8,128)(2,1)}, u32[]{:S(2)}) copy-start(bf16[384,1152]{1,0:T(8,128)(2,1)} %w_ref.1) | copy-start | bytes 2654212
  1.8 1.0 copy-start.1
  2.8 0.7 copy-start.2

commit v4 on v3

--- a/solution.py
+++ b/solution.py
@@ -26,15 +26,15 @@
     return lax.dot_general(a, b, dims, preferred_element_type=F32)
 
 
-def kernel(x_hbm, g_hbm, gain_ref, w_ref, wp_ref, out_ref, qkv_ref, proj_ref,
-           x_ref, g_ref,
+def kernel(x_hbm, g_hbm, gain_hbm, w_hbm, wp_hbm, out_ref, qkv_ref, proj_ref,
+           x_ref, g_ref, gain_ref, w_ref, wp_ref,
            buf, s_a, s_br, s_tl, s_bl, dbuf, ret_tm, ret_br, ret_bl, ret_tl,
            w_t, normed, rstd_s, nl, gs, q_aug, b_aug, k_aug, v_aug, qkv_t, p32, p_low, ds_low, dqkv_t, att_t,
            gp, total, core_send, core_recv, core_own, y_send, y_recv, y_own, lat_send, lat_recv,
            dp_send, dp_recv, send_sems, recv_sems, load_sems):
     dp, xl, z, y, core = (lax.axis_index(n) for n in ("dp", "xl", "z", "y", "core"))
     loads = [pltpu.make_async_copy(src, dst, load_sems.at[n]) for n, (src, dst) in enumerate((
-        (x_hbm.at[0], x_ref), (g_hbm.at[0], g_ref)))]
+        (x_hbm.at[0], x_ref), (g_hbm.at[0], g_ref), (w_hbm, w_ref), (wp_hbm, wp_ref), (gain_hbm, gain_ref)))]
     for load in loads:
         load.start()
     lat = xl * 8 + z
@@ -100,6 +100,8 @@
             buf[1, n, 15 + i, 0:15, :] = ref[i, 45:60, :]
             buf[1, n, 15 + i, 15:16, :] = pad1
 
+    for load in loads[2:]:
+        load.wait()
     gain = gain_ref[...].reshape(1, D)
     for n in range(9):
         w_t[n * 128:(n + 1) * 128, :] = w_ref[:, n * 128:(n + 1) * 128].T
@@ -195,19 +197,13 @@
         arrive(kind, 0)
         clear(kind, 0, edge)
 
-        def norm(n, c):
-            rows = pl.ds(pl.multiple_of(n * 96, 96), 96)
-            cells = pl.ds(n * 3, 3)
-            x = buf[kind, 0, cells].reshape(96, D).astype(F32)
-            centred = x - jnp.sum(x, axis=1, keepdims=True) * (1 / D)
-            rstd = lax.rsqrt(jnp.sum(centred * centred, axis=1, keepdims=True) * (1 / D) + EPS)
-            v = centred * rstd
-            normed[rows, :] = v
-            rstd_s[rows, :] = jnp.broadcast_to(rstd, (96, 128))
-            nl[rows, :] = (v * gain).astype(BF)
-            return c
-
-        lax.fori_loop(0, KC // 96, norm, 0)
+        x = buf[kind, 0].reshape(KC, D).astype(F32)
+        centred = x - jnp.sum(x, axis=1, keepdims=True) * (1 / D)
+        rstd = lax.rsqrt(jnp.sum(centred * centred, axis=1, keepdims=True) * (1 / D) + EPS)
+        v = centred * rstd
+        normed[...] = v
+        rstd_s[...] = jnp.broadcast_to(rstd, (KC, 128))
+        nl[0:KC, :] = (v * gain).astype(BF)
         q = (dot(w_t[0:D, :], nl[...], NT).astype(BF).astype(F32) * 0.125).astype(BF)
         qkv_t[0:6] = q.reshape(6, 64, QC)
         for part in (1, 2):
@@ -296,6 +292,26 @@
     send_y(4, core_own[1, first] + y_recv[0].astype(F32))
     y_copies[1].wait()
     send_y(5, core_own[2, second] + y_recv[1].astype(F32))
+    for n in range(2, 6):
+        y_copies[n].wait()
+    low = core_own[3, first] + y_recv[4].astype(F32) + y_recv[3].astype(F32)
+    high = core_own[3, second] + y_recv[2].astype(F32) + y_recv[5].astype(F32)
+    for n in range(3):
+        y_own[n, first] = low[:, n * 128:(n + 1) * 128]
+        y_own[n, second] = high[:, n * 128:(n + 1) * 128]
+
+    def strided(first):
+        return jnp.concatenate([y_own[n, pl.ds(first, 12, stride=16), :] for n in range(3)], axis=1)
+
+    spare = jnp.zeros((4, D), F32)
+    for t in range(16):
+        lat_send[t] = jnp.concatenate([strided(t), spare], axis=0).astype(BF)
+    lat_copies = []
+    far_first = (4, 12, 3, 5, 11, 13, 2, 6, 10, 14, 1, 7, 9, 15, 8)
+    for k in far_first:
+        c = copy(lat_send.at[lax.rem(lat + k, 16)], lat_recv.at[k - 1], 9 + k, at(k, 0))
+        c.start()
+        lat_copies.append(c)
     back_tm.wait_recv()
     back_br.wait_recv()
     back_bl.wait_recv()
@@ -306,29 +322,10 @@
                 (i, 45, 60, dbuf[1, 15 + i, 0:15, :]), (15 + i, 0, 15, ret_bl[i, 0:15, :]),
                 (15 + i, 15, 45, dbuf[0, i, 0:30, :]), (15 + i, 45, 60, ret_br[i, 0:15, :])):
             out_ref[0, r, c0:c1, :] = (g_ref[r, c0:c1, :].astype(F32) + part.astype(F32)).astype(BF)
-    for n in range(2, 6):
-        y_copies[n].wait()
-    low = core_own[3, first] + y_recv[4].astype(F32) + y_recv[3].astype(F32)
-    high = core_own[3, second] + y_recv[2].astype(F32) + y_recv[5].astype(F32)
-    for n in range(3):
-        y_own[n, first] = low[:, n * 128:(n + 1) * 128]
-        y_own[n, second] = high[:, n * 128:(n + 1) * 128]
-
-    def strided(first):
-        return jnp.concatenate([y_own[n, pl.ds(first, 12, stride=16), :] for n in range(3)], axis=1)
-
-    spare = jnp.zeros((4, D), F32)
-    for t in range(16):
-        lat_send[t] = jnp.concatenate([strided(t), spare], axis=0).astype(BF)
-    lat_copies = []
-    for k in range(1, 16):
-        c = copy(lat_send.at[lax.rem(lat + k, 16)], lat_recv.at[k - 1], 9 + k, at(k, 0))
-        c.start()
-        lat_copies.append(c)
     own = strided(lat)
-    for k in range(15):
-        lat_copies[k].wait()
-        own = own + lat_recv[k, 0:12, :].astype(F32)
+    for c, k in zip(lat_copies, far_first):
+        c.wait()
+        own = own + lat_recv[k - 1, 0:12, :].astype(F32)
     dp_send[...] = jnp.concatenate([own, spare], axis=0)
     c = copy(dp_send, dp_recv, 25, {"dp": 1 - dp})
     c.start()
@@ -345,7 +342,7 @@
 def per_device(hidden_in, grad_out, norm_gain, w_qkv, w_proj):
     V = pl.BlockSpec(memory_space=pltpu.VMEM)
     scratch = [
-        ((30, 60, D), BF), ((30, 60, D), BF),
+        ((30, 60, D), BF), ((30, 60, D), BF), ((D,), F32), ((D, 3 * D), BF), ((D, D), BF),
         ((2, 2, 30, 32, D), BF), ((2, 15, 32, D), BF), ((2, 15, 16, D), BF), ((2, 15, 16, D), BF),
         ((2, 15, 16, D), BF), ((2, 30, 32, D), BF), ((15, 32, D), BF), ((15, 16, D), BF), ((15, 16, D), BF),
         ((15, 16, D), BF),
@@ -357,18 +354,20 @@
         ((16, D), F32), ((16, D), F32),
     ]
     H = pl.BlockSpec(memory_space=pltpu.HBM)
+    args = [pltpu.with_memory_space_constraint(a, pltpu.HBM)
+            for a in (hidden_in, grad_out, norm_gain, w_qkv, w_proj)]
     grad_in, qkv, proj = pl.pallas_call(
         kernel,
         out_shape=(jax.ShapeDtypeStruct(grad_out.shape, BF), jax.ShapeDtypeStruct((9, 192), F32),
                    jax.ShapeDtypeStruct((3, 192), F32)),
-        in_specs=[H, H, V, V, V],
+        in_specs=[H] * 5,
         out_specs=(V, V, V),
         scratch_shapes=[pltpu.VMEM(s, d) for s, d in scratch] + [pltpu.SemaphoreType.DMA((38,))] * 2
-        + [pltpu.SemaphoreType.DMA((2,))],
+        + [pltpu.SemaphoreType.DMA((5,))],
         compiler_params=pltpu.CompilerParams(
             vmem_limit_bytes=50 * 1024 * 1024, collective_id=0, has_side_effects=True),
         name="block_backward",
-    )(hidden_in, grad_out, norm_gain, w_qkv, w_proj)
+    )(*args)
     return grad_in, qkv.T, proj.T
 
 

time: 101 us -> 94.2 us (0.933)
  Pallas kernels: 94.6 us -> 89.9 us
  local copies, waits for them, and re-layouts: 5.11 us -> 2.31 us
    pallas_call x1, Pallas kernels: 94.6 us -> 89.9 us  [per_device(): pl.pallas_call(kernel, out_shape=(jax.ShapeDtypeStruct(grad_out.shape, BF...]
    unnamed x9 -> x3, local copies, waits for them, and re-layouts: 5.11 us -> 2.31 us
where the time goes in v4:
time: 94.2 us; the launch traced here: 92.8 us
  Pallas kernels  89.9 us (95%)
  local copies, waits for them, and re-layouts  2.31 us (2%)
    pallas_call x1, Pallas kernels, per_device(): pl.pallas_call(kernel, out_shape=(jax.ShapeDtypeStruct(grad_out.shape, BF...  89.9 us
    unnamed x3, local copies, waits for them, and re-layouts  2.31 us

profile of v4, /device:TPU:1, one launch (start us, length us, event | category | flops | bytes accessed | tf_op | source)
XLA Modules:
  0.0 92.8 jit_solution(169331202416689210)
XLA Ops:
  0.6 89.9 %block_backward.1 = (bf16[1,30,60,384]{3,2,1,0:T(8,128)(2,1)S(1)}, f32[9,192]{1,0:T(8,128)S(1)}, f32[3,192]{1,0:T(4,128)S(1)}) custom-call(bf16[1,30,60,384]{3,2,1,0:T(8,128)(2,1)} %x_hbm.1, bf16[1,30,60,384]{3,2,1,0:T(8,128)(2,1)} %g_hbm.1, f32[384]{0:T(512)} %gain_hbm.1, bf16[384,1152]{1,0:T(8,128)(2,1)} %w_hbm.1, bf16[384,384]{1,0:T(8,128)(2,1)} %wp_hbm.1), custom_call_target="tpu_custom_call" | custom-call | tf_op jit(solution)/shard_map/block_backward/pallas_call | solution.py:359
  90.5 1.1 %copy.11 = bf16[1,30,60,384]{3,2,1,0:T(8,128)(2,1)} copy(bf16[1,30,60,384]{3,2,1,0:T(8,128)(2,1)S(1)} %get-tuple-element.12) | data formatting | bytes 2764800
  91.6 0.6 copy.12
  92.3 0.6 copy.13

commit v5 on v4

--- a/solution.py
+++ b/solution.py
@@ -126,31 +126,55 @@
     for j in range(3):
         v_aug[j, :, 128:256] = ones
 
-    def head(h, carry):
-        j = h // 2
-        o = pl.multiple_of(lax.rem(h, 2) * 64, 64)
+    def scores(j, u):
         acc = jnp.zeros((8, QC), F32)
         for k in range(0, KC, CK):
-            e = jnp.exp(dot(k_aug[j, k:k + CK, :], q_aug[h]))
-            p32[k:k + CK, :] = e
+            e = jnp.exp(dot(k_aug[j, k:k + CK, :], q_aug[2 * j + u]))
+            p32[u, k:k + CK, :] = e
             acc = acc + jnp.sum(e.reshape(CK // 8, 8, QC), axis=0)
-        r = 1.0 / jnp.sum(acc, axis=0, keepdims=True)
+        return 1.0 / jnp.sum(acc, axis=0, keepdims=True)
+
+    def normalise(u, r):
         for k in range(0, KC, CK):
-            p = p32[k:k + CK, :] * r
-            p32[k:k + CK, :] = p
-            p_low[k:k + CK, :] = p.astype(BF)
-        a = dot(qkv_t[12 + h][:, 0:KC], p_low[...])
+            p = p32[u, k:k + CK, :] * r
+            p32[u, k:k + CK, :] = p
+            p_low[u, k:k + CK, :] = p.astype(BF)
+
+    def attend(j, u):
+        h, o = 2 * j + u, 64 * u
+        a = dot(qkv_t[12 + h][:, 0:KC], p_low[u])
         att_t[h] = a.astype(BF)
-        less = -jnp.sum(a * b_aug[h, pl.ds(o, 64), :].astype(F32), axis=0, keepdims=True)
+        less = -jnp.sum(a * b_aug[h, o:o + 64, :].astype(F32), axis=0, keepdims=True)
         high = less.astype(BF).astype(F32)
         r16 = lax.broadcasted_iota(jnp.int32, (16, QC), 0)
         b_aug[h, 128:144, :] = jnp.where(r16 == 0, high, jnp.where(r16 == 1, less - high, 0.0)).astype(BF)
+
+    def score_grads(j, u):
         for k in range(0, KC, CK):
-            dprobs = dot(v_aug[j, k:k + CK, :], b_aug[h])
-            ds_low[k:k + CK, :] = (p32[k:k + CK, :] * dprobs).astype(BF)
-        dqkv_t[h] = (dot(qkv_t[6 + h][:, 0:KC], ds_low[...]) * 0.125).astype(BF)
-        dqkv_t[6 + h, :, 0:KC] = dot(qkv_t[h], ds_low[...], NT).astype(BF)
-        dqkv_t[12 + h, :, 0:KC] = dot(b_aug[h, pl.ds(o, 64), :], p_low[...], NT).astype(BF)
+            dprobs = dot(v_aug[j, k:k + CK, :], b_aug[2 * j + u])
+            ds_low[u, k:k + CK, :] = (p32[u, k:k + CK, :] * dprobs).astype(BF)
+
+    def value_grads(j, u):
+        h, o = 2 * j + u, 64 * u
+        dqkv_t[12 + h, :, 0:KC] = dot(b_aug[h, o:o + 64, :], p_low[u], NT).astype(BF)
+
+    def query_grads(j, u):
+        h = 2 * j + u
+        dqkv_t[h] = (dot(qkv_t[6 + h][:, 0:KC], ds_low[u]) * 0.125).astype(BF)
+
+    def key_grads(j, u):
+        h = 2 * j + u
+        dqkv_t[6 + h, :, 0:KC] = dot(qkv_t[h], ds_low[u], NT).astype(BF)
+
+    def pair(j, carry):
+        r0 = scores(j, 0)
+        r1 = scores(j, 1)
+        for u, r in ((0, r0), (1, r1)):
+            normalise(u, r)
+            attend(j, u)
+        for step in (score_grads, value_grads, query_grads, key_grads):
+            step(j, 0)
+            step(j, 1)
         return carry
 
     def arrive(kind, n):
@@ -239,7 +263,7 @@
             cols = slice(2 * D + j * 128, 2 * D + (j + 1) * 128)
             v_aug[j, :, 0:128] = dot(nl[0:KC, :], w_ref[:, cols]).astype(BF)
             k_aug[j, :, 128:256] = bias
-        lax.fori_loop(0, HEADS, head, 0)
+        lax.fori_loop(0, HEADS // 2, pair, 0)
         dw = dot(dqkv_t[...].reshape(3 * D, QC), nl[...])
         for n in range(3):
             total[n, 0:1152, :] += dw[:, n * 128:(n + 1) * 128]
@@ -347,8 +371,8 @@
         ((2, 15, 16, D), BF), ((2, 30, 32, D), BF), ((15, 32, D), BF), ((15, 16, D), BF), ((15, 16, D), BF),
         ((15, 16, D), BF),
         ((3 * D, D), BF), ((KC, D), F32), ((KC, 128), F32), ((QC, D), BF), ((QC, D), BF), ((6, 256, QC), BF),
-        ((6, 256, QC), BF), ((3, KC, 256), BF), ((3, KC, 256), BF), ((18, 64, QC), BF), ((KC, QC), F32),
-        ((KC, QC), BF), ((KC, QC), BF), ((18, 64, QC), BF), ((6, 64, QC), BF),
+        ((6, 256, QC), BF), ((3, KC, 256), BF), ((3, KC, 256), BF), ((18, 64, QC), BF), ((2, KC, QC), F32),
+        ((2, KC, QC), BF), ((2, KC, QC), BF), ((18, 64, QC), BF), ((6, 64, QC), BF),
         ((D, D), F32), ((3, 1536, 128), F32), ((4, 192, D), BF), ((4, 192, D), BF), ((4, 192, D), F32),
         ((6, 96, D), BF), ((6, 96, D), BF), ((3, 192, 128), F32), ((16, 16, D), BF), ((15, 16, D), BF),
         ((16, D), F32), ((16, D), F32),
@@ -365,7 +389,7 @@
         scratch_shapes=[pltpu.VMEM(s, d) for s, d in scratch] + [pltpu.SemaphoreType.DMA((38,))] * 2
         + [pltpu.SemaphoreType.DMA((5,))],
         compiler_params=pltpu.CompilerParams(
-            vmem_limit_bytes=50 * 1024 * 1024, collective_id=0, has_side_effects=True),
+            vmem_limit_bytes=52 * 1024 * 1024, collective_id=0, has_side_effects=True),
         name="block_backward",
     )(*args)
     return grad_in, qkv.T, proj.T

time: 94.2 us -> 92 us (0.977)
  Pallas kernels: 89.9 us -> 87.7 us
    pallas_call x1, Pallas kernels: 89.9 us -> 87.7 us  [per_device(): pl.pallas_call(kernel, out_shape=(jax.ShapeDtypeStruct(grad_out.shape, BF...]
where the time goes in v5:
time: 92 us; the launch traced here: 90.6 us
  Pallas kernels  87.7 us (95%)
  local copies, waits for them, and re-layouts  2.31 us (3%)
    pallas_call x1, Pallas kernels, per_device(): pl.pallas_call(kernel, out_shape=(jax.ShapeDtypeStruct(grad_out.shape, BF...  87.7 us
    unnamed x3, local copies, waits for them, and re-layouts  2.31 us

profile of v5, /device:TPU:1, one launch (start us, length us, event | category | flops | bytes accessed | tf_op | source)
XLA Modules:
  0.0 90.6 jit_solution(13257163633734504586)
XLA Ops:
  0.6 87.7 %block_backward.1 = (bf16[1,30,60,384]{3,2,1,0:T(8,128)(2,1)S(1)}, f32[9,192]{1,0:T(8,128)S(1)}, f32[3,192]{1,0:T(4,128)S(1)}) custom-call(bf16[1,30,60,384]{3,2,1,0:T(8,128)(2,1)} %x_hbm.1, bf16[1,30,60,384]{3,2,1,0:T(8,128)(2,1)} %g_hbm.1, f32[384]{0:T(512)} %gain_hbm.1, bf16[384,1152]{1,0:T(8,128)(2,1)} %w_hbm.1, bf16[384,384]{1,0:T(8,128)(2,1)} %wp_hbm.1), custom_call_target="tpu_custom_call" | custom-call | tf_op jit(solution)/shard_map/block_backward/pallas_call | solution.py:383
  88.3 1.1 %copy.11 = bf16[1,30,60,384]{3,2,1,0:T(8,128)(2,1)} copy(bf16[1,30,60,384]{3,2,1,0:T(8,128)(2,1)S(1)} %get-tuple-element.12) | data formatting | bytes 2764800
  89.4 0.6 copy.12
  90.0 0.6 copy.13
